TPU v7x, 128 devices: a whole 4x4x4 slice. The times are simulated.
128 devices in a mesh: blk: 32 (over y_hi, x, z), sub: 4 (over y_lo, core).
Axes of the slice: x: 4, y: 4 (y_hi: 2, y_lo: 2; y = y_hi * 2 + y_lo), z: 4, core: 2. Of those that a mesh axis runs over, the one named last changes fastest.
Arguments:
- source: float32 [5, 32, 64, 8192], P(None, 'sub', None, 'blk'), may hold values from -30 to 30
- inv_diag: float32 [5, 32, 64, 8192], P(None, 'sub', None, 'blk'), may hold values from 0.1 to 0.25
- coupling: float32 [32, 6, 5, 5], P('blk'), may hold values from -0.6 to 0.6
- face_map: int32 [32, 2], replicated, may hold values from 0 to 31, as said below
- wall_jac: float32 [3, 5, 2, 32, 8192], P(None, None, None, 'sub', 'blk'), may hold values from -6 to 6
- ffd_weight: float32 [8, 32, 8192], P(None, 'sub', 'blk'), may hold values from 0.05 to 0.5
- cp_ids: int32 [8, 32, 8192], P(None, 'sub', 'blk'), may hold values from -1 to 49151, as said below
Outputs:
- adjoint: float32 [5, 32, 64, 8192], P(None, 'sub', None, 'blk')
- cp_sens: float32 [3, 49152], P(None, ('blk', 'sub'))
Inputs may be any that keep to these rules, and one draw needn't show every extreme that they name: face_map[b, 0] is the block whose last chordwise cells meet block b's first ones; face_map[b, 1] the block whose first cells meet b's last ones; the second column is the inverse permutation of the first. `cp_ids`: -1 marks an unused slot; any other value is a control point, held by any device; the share of used slots differs from block to block.
All inputs are finite; a program needn't handle non-finite values.
Results may differ from a plain program's by a relative error of at most 0.0001.
Values sent between devices are 32-bit elements; how exact they have to be, the bound alone decides.
A program may use at most 192 MiB of HBM per device.

v0:
```python
import jax
import jax.numpy as jnp
from jax import lax
from jax.sharding import PartitionSpec as P

SWEEPS = 3
CP_DEV = 384


def with_halo(block, sides, width):
    for axis, dim in sides:
        count = lax.axis_size(axis)
        forward = [(i, i + 1) for i in range(count - 1)]
        backward = [(target, source) for source, target in forward]
        low = lax.ppermute(
            lax.slice_in_dim(block, block.shape[dim] - width, None, axis=dim), axis, forward
        )
        high = lax.ppermute(lax.slice_in_dim(block, 0, width, axis=dim), axis, backward)
        block = jnp.concatenate([low, block, high], axis=dim)
    return block


def couple(matrix, field):
    return jnp.einsum("uv,vsni->usni", matrix, field, precision=lax.Precision.HIGHEST)


def relax_piece(adjoint, source, inv_diag, couplings, low_source, high_source):
    padded = with_halo(adjoint, (("sub", 1),), 1)
    chord_ends = jnp.stack([adjoint[..., 0], adjoint[..., -1]], 0)[None]
    all_ends = lax.all_gather(chord_ends, "blk", axis=0, tiled=True)
    low_face = lax.dynamic_index_in_dim(all_ends, low_source, 0, keepdims=False)[1]
    high_face = lax.dynamic_index_in_dim(all_ends, high_source, 0, keepdims=False)[0]
    zero_layer = jnp.zeros((adjoint.shape[0], adjoint.shape[1], 1, adjoint.shape[3]), jnp.float32)
    span_low = padded[:, :-2]
    span_high = padded[:, 2:]
    normal_low = jnp.concatenate([zero_layer, adjoint[:, :, :-1]], 2)
    normal_high = jnp.concatenate([adjoint[:, :, 1:], zero_layer], 2)
    chord_low = jnp.concatenate([low_face[..., None], adjoint[..., :-1]], 3)
    chord_high = jnp.concatenate([adjoint[..., 1:], high_face[..., None]], 3)
    summed = source
    neighbours = [span_low, span_high, normal_low, normal_high, chord_low, chord_high]
    for direction in range(6):
        summed = summed + couple(couplings[direction], neighbours[direction])
    return inv_diag * summed


def body(source, inv_diag, coupling, face_map, wall_jac, ffd_weight, cp_ids):
    couplings = coupling[0]
    block_index = lax.axis_index("blk")
    low_source = face_map[block_index, 0]
    high_source = face_map[block_index, 1]
    adjoint = inv_diag * source
    for sweep_index in range(SWEEPS):
        adjoint = relax_piece(adjoint, source, inv_diag, couplings, low_source, high_source)
    wall_sens = jnp.einsum(
        "cvksi,vski->csi", wall_jac, adjoint[:, :, 0:2, :], precision=lax.Precision.HIGHEST
    )
    contrib = (ffd_weight[None] * wall_sens[:, None]).reshape(3, -1)
    n_blocks = lax.axis_size("blk")
    n_spans = lax.axis_size("sub")
    points_all = CP_DEV * n_blocks * n_spans
    slots = jnp.where(cp_ids < 0, points_all, cp_ids).reshape(-1)

    def one_row(values):
        return jax.ops.segment_sum(values, slots, num_segments=points_all + 1)[:points_all]

    partial_sums = jax.vmap(one_row)(contrib)
    cp_sens = lax.psum_scatter(partial_sums, ("blk", "sub"), scatter_dimension=1, tiled=True)
    return (adjoint, cp_sens)


def solution(mesh):
    in_specs = (
        P(None, "sub", None, "blk"),
        P(None, "sub", None, "blk"),
        P("blk", None, None, None),
        P(),
        P(None, None, None, "sub", "blk"),
        P(None, "sub", "blk"),
        P(None, "sub", "blk"),
    )
    out_specs = (P(None, "sub", None, "blk"), P(None, ("blk", "sub")))
    return jax.shard_map(body, mesh=mesh, in_specs=in_specs, out_specs=out_specs, check_vma=False)
```

profile of v0, /device:TPU:1, one launch (start us, length us, event | category | flops | bytes accessed | tf_op | source)
XLA Modules:
  0.0 1316.6 jit_solution(6364500570921260354)
XLA Ops:
  7.2 5.9 copy_multiply_fusion
  13.1 2.0 copy-done
  15.1 1.1 fusion.121
  16.1 3.3 collective-permute-start.1
  19.5 3.4 collective-permute-start
  22.8 0.7 constant_dynamic-slice_fusion
  26.2 4.4 fusion.123
  30.6 4.8 fusion.122
  35.4 0.2 fusion.124
  35.6 0.1 copy.130
  35.9 0.1 copy.132
  36.0 0.1 copy.131
  36.2 0.1 copy.129
  36.4 8.0 fusion.74
  44.5 5.2 fusion.76
  49.7 2.0 copy.94
  51.7 0.6 copy.95
  52.3 90.4 %all-gather = f32[64,5,8,64]{3,2,1,0:T(8,128)S(1)} all-gather(f32[2,5,8,64]{3,2,1,0:T(8,128)S(1)} %pad_maximum_fusion), channel_id=2, replica_groups=mesh['blk'=32,'sub'=4] {'blk'}, dimensions={0}, use_global_device_ids=true | all-gather | bytes 675840 | tf_op jit(solution)/shard_map/all_gather | solution.py:30
  144.0 2.0 copy.96
  146.0 0.7 copy.98
  146.8 9.2 fusion.42
  156.0 7.1 fusion.46
  163.1 7.0 fusion.3
  170.1 13.3 %copy_multiply_fusion.1 = f32[5,8,64,256]{3,0,2,1:T(8,128)S(1)} fusion(f32[5,8,64,256]{3,2,1,0:T(8,128)S(1)} %copy-done.8, f32[5,8,64,256]{3,2,1,0:T(8,128)S(1)} %copy-done.9, f32[8,64,256,5]{2,3,1,0:T(8,128)} %fusion.46, f32[8,64,256,5]{2,3,1,0:T(8,128)} %fusion.42, f32[8,64,256,5]{2,3,1,0:T(8,128)} %fusion.74, f32[8,64,256,5]{2,3,1,0:T(8,128)} %fusion.76, ...), kind=kOutput, calls=%fused_computation.6 | convolution fusion | flops 44646400 | bytes 23920740 | tf_op jit(solution)/shard_map/uv,vsni->usni/dot_general | solution.py:24
  183.5 1.1 fusion.118
  184.6 5.4 fusion.70
  190.0 5.2 fusion.72
  195.1 2.7 fusion.120
  197.8 4.8 fusion.119
  202.7 15.7 %collective-permute-start.3 = (f32[5,1,64,256]{3,0,2,1:T(8,128)}, f32[5,1,64,256]{3,0,2,1:T(8,128)S(1)}, u32[]{:S(2)}, u32[]{:S(2)}) collective-permute-start(f32[5,1,64,256]{3,0,2,1:T(8,128)} %get-tuple-element.16), channel_id=1, source_target_pairs={{1,0},{2,1},{3,2},{5,4},{6,5},{7,6},{9,8},{10,9},{11,10},{13,12},{... | collective-permute-start | bytes 983048 | tf_op jit(solution)/shard_map/ppermute | solution.py:18
  218.4 1.9 collective-permute-start.2
  220.4 2.0 copy.102
  222.4 2.0 copy.103
  224.5 82.0 %all-gather.1 = f32[64,5,8,64]{3,2,1,0:T(8,128)S(1)} all-gather(f32[2,5,8,64]{3,2,1,0:T(8,128)S(1)} %pad_maximum_fusion.1), channel_id=3, replica_groups=mesh['blk'=32,'sub'=4] {'blk'}, dimensions={0}, use_global_device_ids=true | all-gather | bytes 675840 | tf_op jit(solution)/shard_map/all_gather | solution.py:30
  306.4 2.0 copy.104
  308.4 2.0 copy.105
  310.4 9.2 fusion.50
  319.7 7.1 fusion.54
  326.8 7.1 fusion.11
  333.8 13.3 %copy_multiply_fusion.2 = f32[5,8,64,256]{3,0,2,1:T(8,128)S(1)} fusion(f32[5,8,64,256]{3,2,1,0:T(8,128)S(1)} %copy-done.8, f32[5,8,64,256]{3,2,1,0:T(8,128)S(1)} %copy-done.10, f32[8,64,256,5]{2,3,1,0:T(8,128)} %fusion.54, f32[8,64,256,5]{2,3,1,0:T(8,128)} %fusion.50, f32[8,64,256,5]{2,3,1,0:T(8,128)} %fusion.70, f32[8,64,256,5]{2,3,1,0:T(8,128)} %fusion.72, ...), kind=kOutput, calls=%fused_computation.7 | convolution fusion | flops 44646400 | bytes 23920740 | tf_op jit(solution)/shard_map/uv,vsni->usni/dot_general | solution.py:24
  347.2 1.1 fusion.115
  348.3 5.4 fusion.66
  353.7 5.2 fusion.68
  358.9 2.7 fusion.117
  361.6 4.8 fusion.116
  366.4 16.1 %collective-permute-start.5 = (f32[5,1,64,256]{3,0,2,1:T(8,128)}, f32[5,1,64,256]{3,0,2,1:T(8,128)S(1)}, u32[]{:S(2)}, u32[]{:S(2)}) collective-permute-start(f32[5,1,64,256]{3,0,2,1:T(8,128)} %get-tuple-element.10), channel_id=1, source_target_pairs={{1,0},{2,1},{3,2},{5,4},{6,5},{7,6},{9,8},{10,9},{11,10},{13,12},{... | collective-permute-start | bytes 983048 | tf_op jit(solution)/shard_map/ppermute | solution.py:18
  382.5 1.9 collective-permute-start.4
  384.5 2.0 copy.108
  386.5 2.0 copy.109
  388.6 83.0 %all-gather.2 = f32[64,5,8,64]{3,2,1,0:T(8,128)S(1)} all-gather(f32[2,5,8,64]{3,2,1,0:T(8,128)S(1)} %pad_maximum_fusion.2), channel_id=4, replica_groups=mesh['blk'=32,'sub'=4] {'blk'}, dimensions={0}, use_global_device_ids=true | all-gather | bytes 675840 | tf_op jit(solution)/shard_map/all_gather | solution.py:30
  471.5 2.0 copy.110
  473.5 2.0 copy.111
  475.5 9.2 fusion.58
  484.8 6.9 fusion.62
  491.7 7.1 fusion.19
  498.8 13.4 %copy_multiply_fusion.3 = f32[5,8,64,256]{3,0,2,1:T(8,128)S(1)} fusion(f32[5,8,64,256]{3,2,1,0:T(8,128)S(1)} %copy-done.8, f32[5,8,64,256]{3,2,1,0:T(8,128)S(1)} %copy-done.11, f32[8,64,256,5]{2,3,1,0:T(8,128)} %fusion.62, f32[8,64,256,5]{2,3,1,0:T(8,128)} %fusion.58, f32[8,64,256,5]{2,3,1,0:T(8,128)} %fusion.66, f32[8,64,256,5]{2,3,1,0:T(8,128)} %fusion.68, ...), kind=kOutput, calls=%fused_computation.8 | convolution fusion | flops 44646400 | bytes 23920740 | tf_op jit(solution)/shard_map/uv,vsni->usni/dot_general | solution.py:24
  512.2 2.0 copy-done.12
  514.2 0.4 copy.128
  514.6 4.9 bitcast_multiply_fusion
  519.5 89.6 %scatter_custom_fusion = f32[3,49153]{0,1:T(8,128)} fusion(s32[16384]{0:T(1024)S(1)} %bitcast.152, f32[]{:T(128)} %constant.25.clone.1, f32[3,16384]{0,1:T(8,128)} %bitcast_multiply_fusion), kind=kCustom, calls=%fused_computation.1 | custom fusion | flops 49152 | bytes 786448 | tf_op jit(solution)/shard_map/vmap()/scatter-add | solution.py:65
  609.1 16.8 %slice.231 = f32[3,49152]{0,1:T(8,128)} slice(f32[3,49153]{0,1:T(8,128)} %scatter_custom_fusion), slice={[0:3], [0:49152]} | slice | bytes 1179648 | tf_op jit(solution)/shard_map/vmap()/slice | solution.py:65
  625.9 4.5 copy.113
  630.4 677.4 %reduce-scatter.2.cloned.1.call-done = f32[3,384]{0,1:T(8,128)} async-done(((f32[3,49152]{0,1:T(8,128)}), f32[3,384]{0,1:T(8,128)}) %reduce-scatter.2.cloned.1.call-update) | async-done | bytes 4624 | tf_op jit(solution)/shard_map/reduce_scatter | solution.py:68
  1307.8 1.6 copy.114
  (66 shorter events, 0.6 us)
Async XLA Ops:
  7.2 15.7 %copy-start.22 = (s32[32,2]{0,1:T(2,128)S(1)}, s32[32,2]{0,1:T(2,128)}, u32[]{:S(2)}) copy-start(s32[32,2]{0,1:T(2,128)} %param.10) | copy-start | bytes 772
  7.2 1300.7 %reduce-scatter.2.cloned.1.call-start = ((), (), s32[]{:S(2)}) async-start(), calls=%async_computation.1 | async-start | bytes 25362432 | tf_op jit(solution)/shard_map/reduce_scatter | solution.py:68
  13.1 2.0 copy-start
  16.1 154.0 %collective-permute-start.1 = (f32[5,1,64,256]{3,0,2,1:T(8,128)}, f32[5,1,64,256]{3,0,2,1:T(8,128)S(1)}, u32[]{:S(2)}, u32[]{:S(2)}) collective-permute-start(f32[5,1,64,256]{3,0,2,1:T(8,128)} %get-tuple-element.22), channel_id=1, source_target_pairs={{1,0},{2,1},{3,2},{5,4},{6,5},{7,6},{9,8},{10,9},{11,10},{13,12},{... | collective-permute-start | bytes 983048 | tf_op jit(solution)/shard_map/ppermute | solution.py:18
  19.5 143.6 %collective-permute-start = (f32[5,1,64,256]{3,0,2,1:T(8,128)}, f32[5,1,64,256]{3,0,2,1:T(8,128)}, u32[]{:S(2)}, u32[]{:S(2)}) collective-permute-start(f32[5,1,64,256]{3,0,2,1:T(8,128)} %get-tuple-element.23), channel_id=1, source_target_pairs={{0,1},{1,2},{2,3},{4,5},{5,6},{6,7},{8,9},{9,10},{10,11},{12,13},{... | collective-permute-start | bytes 983048 | tf_op jit(solution)/shard_map/ppermute | solution.py:15
  26.2 4.4 copy-start.1
  30.6 4.8 copy-start.20
  30.6 4.8 copy-start.21
  30.6 4.9 copy-start.18
  36.4 8.0 copy-start.2
  146.8 9.3 copy-start.13
  156.0 7.1 copy-start.3
  163.1 7.0 copy-start.8
  163.1 7.0 copy-start.9
  183.5 14.4 %copy-start.6 = (f32[5,8,64,256]{3,0,2,1:T(8,128)}, f32[5,8,64,256]{3,0,2,1:T(8,128)S(1)}, u32[]{:S(2)}) copy-start(f32[5,8,64,256]{3,0,2,1:T(8,128)S(1)} %copy_multiply_fusion.1) | copy-start | bytes 7864324
  202.7 131.2 %collective-permute-start.3 = (f32[5,1,64,256]{3,0,2,1:T(8,128)}, f32[5,1,64,256]{3,0,2,1:T(8,128)S(1)}, u32[]{:S(2)}, u32[]{:S(2)}) collective-permute-start(f32[5,1,64,256]{3,0,2,1:T(8,128)} %get-tuple-element.16), channel_id=1, source_target_pairs={{1,0},{2,1},{3,2},{5,4},{6,5},{7,6},{9,8},{10,9},{11,10},{13,12},{... | collective-permute-start | bytes 983048 | tf_op jit(solution)/shard_map/ppermute | solution.py:18
  218.4 108.3 %collective-permute-start.2 = (f32[5,1,64,256]{3,0,2,1:T(8,128)}, f32[5,1,64,256]{3,0,2,1:T(8,128)}, u32[]{:S(2)}, u32[]{:S(2)}) collective-permute-start(f32[5,1,64,256]{3,0,2,1:T(8,128)} %get-tuple-element.17), channel_id=1, source_target_pairs={{0,1},{1,2},{2,3},{4,5},{5,6},{6,7},{8,9},{9,10},{10,11},{12,13},{... | collective-permute-start | bytes 983048 | tf_op jit(solution)/shard_map/ppermute | solution.py:15
  310.4 9.2 copy-start.15
  310.4 9.2 copy-start.17
  319.7 7.1 copy-start.7
  326.8 7.1 copy-start.10
  347.2 14.4 %copy-start.4 = (f32[5,8,64,256]{3,0,2,1:T(8,128)}, f32[5,8,64,256]{3,0,2,1:T(8,128)S(1)}, u32[]{:S(2)}) copy-start(f32[5,8,64,256]{3,0,2,1:T(8,128)S(1)} %copy_multiply_fusion.2) | copy-start | bytes 7864324
  366.4 132.4 %collective-permute-start.5 = (f32[5,1,64,256]{3,0,2,1:T(8,128)}, f32[5,1,64,256]{3,0,2,1:T(8,128)S(1)}, u32[]{:S(2)}, u32[]{:S(2)}) collective-permute-start(f32[5,1,64,256]{3,0,2,1:T(8,128)} %get-tuple-element.10), channel_id=1, source_target_pairs={{1,0},{2,1},{3,2},{5,4},{6,5},{7,6},{9,8},{10,9},{11,10},{13,12},{... | collective-permute-start | bytes 983048 | tf_op jit(solution)/shard_map/ppermute | solution.py:18
  382.5 109.1 %collective-permute-start.4 = (f32[5,1,64,256]{3,0,2,1:T(8,128)}, f32[5,1,64,256]{3,0,2,1:T(8,128)}, u32[]{:S(2)}, u32[]{:S(2)}) collective-permute-start(f32[5,1,64,256]{3,0,2,1:T(8,128)} %get-tuple-element.11), channel_id=1, source_target_pairs={{0,1},{1,2},{2,3},{4,5},{5,6},{6,7},{8,9},{9,10},{10,11},{12,13},{... | collective-permute-start | bytes 983048 | tf_op jit(solution)/shard_map/ppermute | solution.py:15
  475.5 9.2 copy-start.14
  475.5 9.2 copy-start.16
  484.8 6.9 copy-start.5
  491.7 7.1 copy-start.11
  498.8 15.4 %copy-start.19 = (f32[3,5,2,8,256]{4,3,2,1,0:T(8,128)S(1)}, f32[3,5,2,8,256]{4,3,2,1,0:T(8,128)}, u32[]{:S(2)}) copy-start(f32[3,5,2,8,256]{4,3,2,1,0:T(8,128)} %param.11) | copy-start | bytes 737284
  512.1 2.0 copy-start.12
Sparse Core Ops, SparseCore 0:
  626.0 681.7 reduce-scatter.1
where the time goes:
time: 1330 us; the launch traced here: 1320 us
  waiting for transfers between devices  677 us (51%)
  blocking collectives  255 us (19%)
  matrix products  144 us (11%)
  other arithmetic  100 us (8%)
  local copies, waits for them, and re-layouts  78.1 us (6%)
  starting transfers between devices  42.4 us (3%)
  between operations  18.6 us (1%)
    reduce_scatter x1, waiting for transfers between devices, body(): lax.psum_scatter(partial_sums, ('blk', 'sub'), scatter_dimension=1, tiled...  677 us
    all_gather x3, blocking collectives, relax_piece(): all_ends = lax.all_gather(chord_ends, 'blk', axis=0, tiled=True)  255 us
    dot_general x18, matrix products, couple(): jnp.einsum('uv,vsni->usni', matrix, field, precision=lax.Precision.HIGHEST)  144 us
    scatter-add x1, other arithmetic, one_row(): jax.ops.segment_sum(values, slots, num_segments=points_all + 1)[:points_all]  89.6 us
    ppermute x3, starting transfers between devices, with_halo(): lax.ppermute(lax.slice_in_dim(block, 0, width, axis=dim), axis, backward)  35.2 us
  transfers between devices with their start and end apart: 7, of which 1 were waited for; matrix products, arithmetic and copies ran while one was open for 9% of the time, Pallas kernels for 0%

commit v1 on v0

v1 whole, which is shorter than its diff:
```python
import functools

import jax
import jax.numpy as jnp
from jax import lax
from jax.experimental import pallas as pl
from jax.experimental.pallas import tpu as pltpu
from jax.sharding import PartitionSpec as P

MESH = pl.DeviceIdType.MESH
NVAR = 5
CS = 8
CK = 64
CI = 256
SWEEPS = 3
NBLK = 32
NSUB = 4
KT = CK // 8


def face_lane(half, tile, row):
    return half * 64 + tile * 8 + row


def place(lane, value, source_lane, target_lane, into):
    shift = lax.rem(target_lane - source_lane + 128, 128)
    return jnp.where(lane == target_lane, pltpu.roll(value, shift, 1), into)


def relax_row(s, p, q, q_pad, coup, src, invd, packed):
    row = lax.broadcasted_iota(jnp.int32, (8, CI), 0)
    lane = lax.broadcasted_iota(jnp.int32, (8, CI), 1)
    lane1 = lax.broadcasted_iota(jnp.int32, (8, 128), 1)
    zero = jnp.zeros((8, CI), jnp.float32)
    packed = list(packed)
    below = [zero] * NVAR
    here = [p[v, s + 1, 0:8, :] for v in range(NVAR)]
    here_up = [pltpu.roll(x, 7, 0) for x in here]
    for t in range(KT):
        rows = slice(8 * t, 8 * t + 8)
        if t < KT - 1:
            after = [p[v, s + 1, 8 * t + 8 : 8 * t + 16, :] for v in range(NVAR)]
            after_up = [pltpu.roll(x, 7, 0) for x in after]
        else:
            after, after_up = None, [zero] * NVAR
        acc = [src[u, s, rows, :] for u in range(NVAR)]
        for v in range(NVAR):
            x = here[v]
            down = pltpu.roll(x, 1, 0)
            nbs = (
                p[v, s, rows, :],
                p[v, s + 2, rows, :],
                jnp.where(row == 0, below[v], down),
                jnp.where(row == 7, after_up[v], here_up[v]),
                jnp.where(lane == 0, 0.0, pltpu.roll(x, 1, 1)),
                jnp.where(lane == CI - 1, 0.0, pltpu.roll(x, CI - 1, 1)),
            )
            below[v] = down
            for d in range(6):
                for u in range(NVAR):
                    acc[u] = acc[u] + coup[d * 25 + u * 5 + v] * nbs[d]
        for u in range(NVAR):
            value = invd[u, s, rows, :] * acc[u]
            q[u, s + q_pad, rows, :] = value
            if packed:
                both = place(lane1, value[:, 128:], 127, face_lane(0, t, s), packed[u])
                packed[u] = place(lane1, value[:, :128], 0, face_lane(1, t, s), both)
        here, here_up = after, after_up
    return tuple(packed)


def sweep_kernel(coup, fmap, src, invd, wjac, out, wall, p0, p1, p2, fsend, fbuf0, fbuf1, fbuf2, fs_sem, fr_sem, hs_sem, hr_sem):
    blk = lax.axis_index("blk")
    sub = lax.axis_index("sub")
    lane1 = lax.broadcasted_iota(jnp.int32, (8, 128), 1)
    fields = (p0, p1, p2)
    fbufs = (fbuf0, fbuf1, fbuf2)

    barrier = pltpu.get_barrier_semaphore()

    def greet(d, c):
        pl.semaphore_signal(barrier, inc=1, device_id=(lax.rem(blk + d, NBLK), sub), device_id_type=MESH)
        return c

    lax.fori_loop(1, NBLK, greet, 0)
    for step in (1, 3):
        pl.semaphore_signal(barrier, inc=1, device_id=(blk, lax.rem(sub + step, NSUB)), device_id_type=MESH)

    def first_row(s, packed):
        face, diag = list(packed[:NVAR]), list(packed[NVAR:])
        for v in range(NVAR):
            for t in range(KT):
                rows = slice(8 * t, 8 * t + 8)
                inv = invd[v, s, rows, :]
                value = inv * src[v, s, rows, :]
                p0[v, s + 1, rows, :] = value
                face[v] = place(lane1, value[:, 128:], 127, face_lane(0, t, s), face[v])
                face[v] = place(lane1, value[:, :128], 0, face_lane(1, t, s), face[v])
                diag[v] = place(lane1, inv[:, :128], 0, face_lane(0, t, s), diag[v])
                diag[v] = place(lane1, inv[:, 128:], 127, face_lane(1, t, s), diag[v])
        return tuple(face + diag)

    none = jnp.zeros((8, 128), jnp.float32)
    packed = lax.fori_loop(0, CS, first_row, (none,) * (2 * NVAR))
    face, diag = packed[:NVAR], packed[NVAR:]

    @pl.when(sub == 0)
    def _():
        for p in fields:
            p[:, 0] = jnp.zeros((NVAR, CK, CI), jnp.float32)

    @pl.when(sub == NSUB - 1)
    def _():
        for p in fields:
            p[:, CS + 1] = jnp.zeros((NVAR, CK, CI), jnp.float32)

    pl.semaphore_wait(barrier, NBLK - 1 + 2)

    def up_copy(n):
        return pltpu.make_async_remote_copy(
            src_ref=fields[n].at[:, CS], dst_ref=fields[n].at[:, 0], send_sem=hs_sem.at[n, 0], recv_sem=hr_sem.at[n, 0],
            device_id=(blk, lax.rem(sub + 1, NSUB)), device_id_type=MESH)

    def down_copy(n):
        return pltpu.make_async_remote_copy(
            src_ref=fields[n].at[:, 1], dst_ref=fields[n].at[:, CS + 1], send_sem=hs_sem.at[n, 1], recv_sem=hr_sem.at[n, 1],
            device_id=(blk, lax.rem(sub + NSUB - 1, NSUB)), device_id_type=MESH)

    for n in range(SWEEPS):
        p = fields[n]
        fbuf = fbufs[n]
        last = n == SWEEPS - 1
        q, q_pad = (out, 0) if last else (fields[n + 1], 1)

        for v in range(NVAR):
            fsend[n, v] = face[v]
            fbuf[blk, v] = face[v]

        def send_face(d, c):
            target = lax.rem(blk + d, NBLK)
            pltpu.make_async_remote_copy(
                src_ref=fsend.at[n], dst_ref=fbuf.at[blk], send_sem=fs_sem.at[n], recv_sem=fr_sem.at[n],
                device_id=(target, sub), device_id_type=MESH).start()
            return c

        lax.fori_loop(1, NBLK, send_face, 0, unroll=31)

        if n > 0:
            def add_faces(s, c):
                for u in range(NVAR):
                    for t in range(KT):
                        rows = slice(8 * t, 8 * t + 8)
                        low = place(lane1, extra[u], face_lane(0, t, s), 0, 0.0)
                        high = place(lane1, extra[u], face_lane(1, t, s), 127, 0.0)
                        p[u, s + 1, rows, 0:128] = p[u, s + 1, rows, 0:128] + low
                        p[u, s + 1, rows, 128:256] = p[u, s + 1, rows, 128:256] + high
                return c

            lax.fori_loop(0, 2, lambda i, c: add_faces(i * (CS - 1), c), 0)
        pl.when(sub < NSUB - 1)(lambda: up_copy(n).start())
        pl.when(sub > 0)(lambda: down_copy(n).start())
        if n > 0:
            lax.fori_loop(1, CS - 1, add_faces, 0)

        faces0 = () if last else (none,) * NVAR
        step = lambda s, c: relax_row(s, p, q, q_pad, coup, src, invd, c)
        faces0 = lax.fori_loop(1, CS - 1, step, faces0)
        pl.when(sub > 0)(lambda: up_copy(n).wait_recv())
        pl.when(sub < NSUB - 1)(lambda: down_copy(n).wait_recv())
        faces0 = lax.fori_loop(0, 2, lambda i, c: step(i * (CS - 1), c), faces0)

        landed = fbuf.at[pl.ds(0, NBLK - 1)]
        pltpu.make_async_copy(landed, landed, fr_sem.at[n]).wait()
        low = fbuf[fmap[2 * blk]]
        high = fbuf[fmap[2 * blk + 1]]
        from_low = lane1 < 64
        outer = [jnp.where(from_low, low[v], high[v]) for v in range(NVAR)]
        extra = []
        for u in range(NVAR):
            total = none
            for v in range(NVAR):
                total = total + jnp.where(from_low, coup[100 + u * 5 + v], coup[125 + u * 5 + v]) * outer[v]
            extra.append(diag[u] * total)
        if not last:
            face = [faces0[u] + pltpu.roll(extra[u], 64, 1) for u in range(NVAR)]

    def add_last(s, c):
        for u in range(NVAR):
            for t in range(KT):
                rows = slice(8 * t, 8 * t + 8)
                low = place(lane1, extra[u], face_lane(0, t, s), 0, 0.0)
                high = place(lane1, extra[u], face_lane(1, t, s), 127, 0.0)
                out[u, s, rows, 0:128] = out[u, s, rows, 0:128] + low
                out[u, s, rows, 128:256] = out[u, s, rows, 128:256] + high
        return c

    lax.fori_loop(0, CS, add_last, 0)
    for c in range(3):
        total = jnp.zeros((CS, CI), jnp.float32)
        for v in range(NVAR):
            for k in range(2):
                total = total + wjac[c, v, k] * out[v, :, k, :]
        wall[c] = total

    for n in range(SWEEPS):
        pl.when(sub < NSUB - 1)(lambda n=n: up_copy(n).wait_send())
        pl.when(sub > 0)(lambda n=n: down_copy(n).wait_send())
        sent = fbufs[n].at[pl.ds(0, NBLK - 1)]
        pltpu.make_async_copy(sent, sent, fs_sem.at[n]).wait()


def sweeps(source, inv_diag, coupling, face_map, wall_jac):
    vmem = pl.BlockSpec(memory_space=pltpu.VMEM)
    smem = pl.BlockSpec(memory_space=pltpu.SMEM)
    return pl.pallas_call(
        sweep_kernel,
        out_shape=(
            jax.ShapeDtypeStruct((NVAR, CS, CK, CI), jnp.float32),
            jax.ShapeDtypeStruct((3, CS, CI), jnp.float32),
        ),
        in_specs=[smem, smem, vmem, vmem, vmem],
        out_specs=(vmem, vmem),
        scratch_shapes=[pltpu.VMEM((NVAR, CS + 2, CK, CI), jnp.float32)] * 3
        + [
            pltpu.VMEM((SWEEPS, NVAR, 8, 128), jnp.float32),
            pltpu.VMEM((NBLK, NVAR, 8, 128), jnp.float32),
            pltpu.VMEM((NBLK, NVAR, 8, 128), jnp.float32),
            pltpu.VMEM((NBLK, NVAR, 8, 128), jnp.float32),
            pltpu.SemaphoreType.DMA((SWEEPS,)),
            pltpu.SemaphoreType.DMA((SWEEPS,)),
            pltpu.SemaphoreType.DMA((SWEEPS, 2)),
            pltpu.SemaphoreType.DMA((SWEEPS, 2)),
        ],
        compiler_params=pltpu.CompilerParams(collective_id=0, has_side_effects=True, vmem_limit_bytes=44 << 20),
        name="sweeps",
    )(coupling.reshape(-1), face_map.reshape(-1), source, inv_diag, wall_jac)


SLOT_TILE = 2048


def scatter_kernel(wall, weight, ids, dense, onehot, spread):
    m = pl.program_id(0)

    point = ids[0]
    high = point >> 7
    holder = (high * 171) >> 9
    order = (holder & 1) * 64 + (holder >> 1)
    rank = jnp.where(point < 0, -1, (high - 3 * holder) * 128 + order)
    low = point & 127
    pieces = []
    for c in range(3):
        value = weight[0] * wall[c]
        top = value.astype(jnp.bfloat16).astype(jnp.float32)
        pieces.append(top)
        pieces.append(value - top)
    for s in range(CS):
        lanes = slice(s * CI, (s + 1) * CI)
        hit = lax.broadcasted_iota(jnp.int32, (384, CI), 0) == rank[s : s + 1, :]
        onehot[:, lanes] = jnp.where(hit, 1.0, 0.0).astype(jnp.bfloat16)
        match = lax.broadcasted_iota(jnp.int32, (128, CI), 0) == low[s : s + 1, :]
        for i in range(6):
            spread[i * 128 : (i + 1) * 128, lanes] = jnp.where(match, pieces[i][s : s + 1, :], 0.0).astype(jnp.bfloat16)
    for j in range(3):
        part = lax.dot_general(
            onehot[j * 128 : (j + 1) * 128, :], spread[...], (((1,), (1,)), ((), ())), preferred_element_type=jnp.float32)
        for c in range(3):
            total = part[:, c * 256 : c * 256 + 128] + part[:, c * 256 + 128 : c * 256 + 256]
            for g in range(16):
                at = pl.ds(g * 128 + c * 3 + j, 8, stride=16)
                piece = total[g * 8 : g * 8 + 8, :]

                @pl.when(m == 0)
                def _():
                    dense[at, :] = piece

                @pl.when(m > 0)
                def _():
                    dense[at, :] = dense[at, :] + piece


def scatter(wall, weight, ids):
    return pl.pallas_call(
        scatter_kernel,
        grid=(8,),
        out_shape=jax.ShapeDtypeStruct((2048, 128), jnp.float32),
        in_specs=[
            pl.BlockSpec((3, CS, CI), lambda m: (0, 0, 0)),
            pl.BlockSpec((1, CS, CI), lambda m: (m, 0, 0)),
            pl.BlockSpec((1, CS, CI), lambda m: (m, 0, 0)),
        ],
        out_specs=pl.BlockSpec((2048, 128), lambda m: (0, 0)),
        scratch_shapes=[pltpu.VMEM((384, SLOT_TILE), jnp.bfloat16), pltpu.VMEM((768, SLOT_TILE), jnp.bfloat16)],
        compiler_params=pltpu.CompilerParams(vmem_limit_bytes=40 << 20),
        name="scatter",
    )(wall, weight, ids)


def holder_kernel(dense, out, pair, mine, landing, sems, fs_sem, fr_sem):
    blk = lax.axis_index("blk")
    sub = lax.axis_index("sub")
    side, core = sub // 2, lax.rem(sub, 2)
    chip = blk * 2 + side

    def device(other):
        return (other // 2, lax.rem(other, 2) * 2 + core)

    partner = (blk, side * 2 + 1 - core)
    barrier = pltpu.get_barrier_semaphore()

    def greet(d, c):
        pl.semaphore_signal(barrier, inc=1, device_id=device(lax.rem(chip + d, 64)), device_id_type=MESH)
        return c

    lax.fori_loop(1, 64, greet, 0)
    pl.semaphore_signal(barrier, inc=1, device_id=partner, device_id_type=MESH)
    pl.semaphore_wait(barrier, 64)

    swap = pltpu.make_async_remote_copy(
        src_ref=dense.at[pl.ds((1 - core) * 64, 64)], dst_ref=pair, send_sem=sems.at[0], recv_sem=sems.at[1],
        device_id=partner, device_id_type=MESH)
    swap.start()
    swap.wait()

    def add(i, c):
        at = pl.ds(i * 8, 8)
        mine[at] = dense[pl.ds(core * 64 + i * 8, 8)] + pair[at]
        return c

    lax.fori_loop(0, 8, add, 0)

    def send(d, c):
        other = lax.rem(chip + d, 64)
        pltpu.make_async_remote_copy(
            src_ref=mine.at[other], dst_ref=landing.at[d], send_sem=fs_sem, recv_sem=fr_sem,
            device_id=device(other), device_id_type=MESH).start()
        return c

    lax.fori_loop(1, 64, send, 0, unroll=9)
    landing[0] = mine[chip]
    landed = landing.at[pl.ds(1, 63)]
    pltpu.make_async_copy(landed, landed, fr_sem).wait()

    def total(i, acc):
        return acc + landing[i]

    acc = lax.fori_loop(0, 64, total, jnp.zeros((16, 128), jnp.float32), unroll=8)
    for c in range(3):
        for j in range(3):
            out[c : c + 1, j * 128 : (j + 1) * 128] = acc[c * 3 + j : c * 3 + j + 1, :]
    pltpu.make_async_copy(landed, landed, fs_sem).wait()


def to_holders(dense):
    vmem = pl.BlockSpec(memory_space=pltpu.VMEM)
    return pl.pallas_call(
        holder_kernel,
        out_shape=jax.ShapeDtypeStruct((3, 384), jnp.float32),
        in_specs=[vmem],
        out_specs=vmem,
        scratch_shapes=[
            pltpu.VMEM((64, 16, 128), jnp.float32),
            pltpu.VMEM((64, 16, 128), jnp.float32),
            pltpu.VMEM((64, 16, 128), jnp.float32),
            pltpu.SemaphoreType.DMA((2,)),
            pltpu.SemaphoreType.DMA,
            pltpu.SemaphoreType.DMA,
        ],
        compiler_params=pltpu.CompilerParams(collective_id=1, has_side_effects=True),
        name="to_holders",
    )(dense.reshape(128, 16, 128))


def body(source, inv_diag, coupling, face_map, wall_jac, ffd_weight, cp_ids):
    adjoint, wall = sweeps(source, inv_diag, coupling[0], face_map, wall_jac)
    dense = scatter(wall, ffd_weight, cp_ids)
    return adjoint, to_holders(dense)


def solution(mesh):
    in_specs = (
        P(None, "sub", None, "blk"),
        P(None, "sub", None, "blk"),
        P("blk", None, None, None),
        P(),
        P(None, None, None, "sub", "blk"),
        P(None, "sub", "blk"),
        P(None, "sub", "blk"),
    )
    out_specs = (P(None, "sub", None, "blk"), P(None, ("blk", "sub")))
    return jax.shard_map(body, mesh=mesh, in_specs=in_specs, out_specs=out_specs, check_vma=False)
```

time: 1330 us -> 128 us (0.10)
  waiting for transfers between devices: 677 us -> 0 us
  blocking collectives: 255 us -> 0 us
  matrix products: 144 us -> 0 us
  Pallas kernels: 0 us -> 118 us
  other arithmetic: 100 us -> 0 us
  local copies, waits for them, and re-layouts: 78.1 us -> 9.29 us
  starting transfers between devices: 42.4 us -> 0 us
  between operations: 18.6 us -> 0.7 us
    reduce_scatter x1 -> x0, waiting for transfers between devices: 677 us -> none  [body(): lax.psum_scatter(partial_sums, ('blk', 'sub'), scatter_dimension=1, tiled...]
    all_gather x3 -> x0, blocking collectives: 255 us -> none  [relax_piece(): all_ends = lax.all_gather(chord_ends, 'blk', axis=0, tiled=True)]
    dot_general x18 -> x0, matrix products: 144 us -> none  [couple(): jnp.einsum('uv,vsni->usni', matrix, field, precision=lax.Precision.HIGHEST)]
    pallas_call x0 -> x3, Pallas kernels: none -> 118 us  [the longest x1 55.7 us: sweeps(): pl.pallas_call(sweep_kernel, out_shape=(jax.ShapeDtypeStruct((NVAR, CS, C...]
    scatter-add x1 -> x0, other arithmetic: 89.6 us -> none  [one_row(): jax.ops.segment_sum(values, slots, num_segments=points_all + 1)[:points_all]]
    slice x17 -> x0, local copies, waits for them, and re-layouts: 55.3 us -> none  [the longest x9 20.6 us: relax_piece(): chord_ends = jnp.stack([adjoint[..., 0], adjoint[..., -1]], 0)[None]]
    ppermute x6 -> x0, starting transfers between devices: 42.4 us -> none  [the longest x3 35.2 us: with_halo(): lax.ppermute(lax.slice_in_dim(block, 0, width, axis=dim), axis, backward)]
  transfers between devices with their start and end apart: 7 -> 0, of which waited for: 1 -> 0; matrix products, arithmetic and copies ran while one was open for 9% -> 0% of each run, Pallas kernels for 0% -> 0%
where the time goes in v1:
time: 128 us
  Pallas kernels  118 us (92%)
  local copies, waits for them, and re-layouts  9.29 us (7%)
    pallas_call x1, Pallas kernels, sweeps(): pl.pallas_call(sweep_kernel, out_shape=(jax.ShapeDtypeStruct((NVAR, CS, C...  55.7 us
    pallas_call x1, Pallas kernels, scatter(): pl.pallas_call(scatter_kernel, grid=(8,), out_shape=jax.ShapeDtypeStruct(...  46.5 us
    pallas_call x1, Pallas kernels, to_holders(): pl.pallas_call(holder_kernel, out_shape=jax.ShapeDtypeStruct((3, 384), jn...  15.6 us
    unnamed x18, local copies, waits for them, and re-layouts  9.09 us

profile of v1, /device:TPU:1, one launch (start us, length us, event | category | flops | bytes accessed | tf_op | source)
XLA Modules:
  0.0 127.7 jit_solution(16311915061758578584)
XLA Ops:
  0.6 0.8 copy.11
  1.4 0.1 reshape.10.fmap
  1.5 0.8 copy.10
  2.3 0.1 reshape_squeeze.3.coup
  2.4 0.0 copy-start.1
  2.5 1.7 %copy-done.1 = f32[5,8,64,256]{3,2,1,0:T(8,128)S(1)} copy-done((f32[5,8,64,256]{3,2,1,0:T(8,128)S(1)}, f32[5,8,64,256]{3,2,1,0:T(8,128)}, u32[]{:S(2)}) %copy-start.1) | copy-done | bytes 2621464
  4.2 0.0 copy-start.2
  4.2 1.7 %copy-done.2 = f32[5,8,64,256]{3,2,1,0:T(8,128)S(1)} copy-done((f32[5,8,64,256]{3,2,1,0:T(8,128)S(1)}, f32[5,8,64,256]{3,2,1,0:T(8,128)}, u32[]{:S(2)}) %copy-start.2) | copy-done | bytes 2621464
  5.9 0.0 copy-start.3
  5.9 0.9 copy-done.3
  6.9 0.0 copy-start.4
  6.9 0.0 copy-start.5
  6.9 55.7 %sweeps.1 = (f32[5,8,64,256]{3,2,1,0:T(8,128)S(1)}, f32[3,8,256]{2,1,0:T(8,128)S(1)}) custom-call(f32[150]{0:T(256)S(1)} %reshape_squeeze.3.coup, s32[64]{0:T(128)S(1)} %reshape.10.fmap, f32[5,8,64,256]{3,2,1,0:T(8,128)S(1)} %copy-done.1, f32[5,8,64,256]{3,2,1,0:T(8,128)S(1)} %copy-done.2, f32[3,5,2,8,256]{4,3,2,1,0:T(8,128)S(1)} %copy-done.3), custom_call_target="tpu_custom_call" | custom-call | tf_op jit(solution)/shard_map/sweeps/pallas_call | solution.py:215
  62.6 0.0 copy-done.4
  62.6 0.0 copy-done.5
  62.6 46.5 %scatter.1 = f32[2048,128]{1,0:T(8,128)S(1)} custom-call(f32[3,8,256]{2,1,0:T(8,128)S(1)} %get-tuple-element.5.wall, f32[8,8,256]{2,1,0:T(8,128)S(1)} %copy-done.4, s32[8,8,256]{2,1,0:T(8,128)S(1)} %copy-done.5), custom_call_target="tpu_custom_call" | custom-call | tf_op jit(solution)/shard_map/scatter/pallas_call | solution.py:283
  109.0 0.0 copy-start
  109.0 1.0 copy-done
  110.0 15.6 %to_holders.1 = f32[3,384]{1,0:T(4,128)} custom-call(f32[128,16,128]{2,1,0:T(8,128)} %bitcast.1), custom_call_target="tpu_custom_call" | custom-call | tf_op jit(solution)/shard_map/to_holders/pallas_call | solution.py:356
  125.6 0.0 copy-start.6
  125.6 1.5 %copy.14 = f32[5,8,64,256]{3,2,1,0:T(8,128)} copy(f32[5,8,64,256]{3,2,1,0:T(8,128)S(1)} %get-tuple-element.8) | data formatting | bytes 5242880
  127.1 0.0 copy-done.6
  127.1 0.6 copy.15
Async XLA Ops:
  2.4 1.7 %copy-start.1 = (f32[5,8,64,256]{3,2,1,0:T(8,128)S(1)}, f32[5,8,64,256]{3,2,1,0:T(8,128)}, u32[]{:S(2)}) copy-start(f32[5,8,64,256]{3,2,1,0:T(8,128)} %src.1) | copy-start | bytes 7864324
  4.2 1.7 %copy-start.2 = (f32[5,8,64,256]{3,2,1,0:T(8,128)S(1)}, f32[5,8,64,256]{3,2,1,0:T(8,128)}, u32[]{:S(2)}) copy-start(f32[5,8,64,256]{3,2,1,0:T(8,128)} %invd.1) | copy-start | bytes 7864324
  5.9 0.9 copy-start.3
  6.9 55.7 %copy-start.4 = (f32[8,8,256]{2,1,0:T(8,128)S(1)}, f32[8,8,256]{2,1,0:T(8,128)}, u32[]{:S(2)}) copy-start(f32[8,8,256]{2,1,0:T(8,128)} %weight.1) | copy-start | bytes 196612
  6.9 55.7 %copy-start.5 = (s32[8,8,256]{2,1,0:T(8,128)S(1)}, s32[8,8,256]{2,1,0:T(8,128)}, u32[]{:S(2)}) copy-start(s32[8,8,256]{2,1,0:T(8,128)} %ids.1) | copy-start | bytes 196612
  109.0 1.0 copy-start
  125.6 1.5 %copy-start.6 = (f32[3,384]{1,0:T(4,128)S(1)}, f32[3,384]{1,0:T(4,128)}, u32[]{:S(2)}) copy-start(f32[3,384]{1,0:T(4,128)} %to_holders.1) | copy-start | bytes 13828

commit v2 on v1

v2 whole, which is shorter than its diff:
```python
import functools

import jax
import jax.numpy as jnp
from jax import lax
from jax.experimental import pallas as pl
from jax.experimental.pallas import tpu as pltpu
from jax.sharding import PartitionSpec as P

MESH = pl.DeviceIdType.MESH
NVAR = 5
CS = 8
CK = 64
CI = 256
SWEEPS = 3
NBLK = 32
NSUB = 4
KT = CK // 8
HALVES = (slice(0, 128), slice(128, 256))


def face_lane(half, tile, row):
    return half * 64 + tile * 8 + row


def place(lane, value, source_lane, target_lane, into):
    shift = lax.rem(target_lane - source_lane + 128, 128)
    return jnp.where(lane == target_lane, pltpu.roll(value, shift, 1), into)


def relax_row(s, p, q, q_pad, coef, src, invd, packed):
    row = lax.broadcasted_iota(jnp.int32, (8, 128), 0)
    lane = lax.broadcasted_iota(jnp.int32, (8, 128), 1)
    zero = jnp.zeros((8, 128), jnp.float32)
    packed = list(packed)
    below = [[zero, zero] for _ in range(NVAR)]
    here = [[p[v, s + 1, 0:8, h] for h in HALVES] for v in range(NVAR)]
    here_up = [[pltpu.roll(x, 7, 0) for x in pair] for pair in here]
    for t in range(KT):
        rows = slice(8 * t, 8 * t + 8)
        if t < KT - 1:
            after = [[p[v, s + 1, 8 * t + 8 : 8 * t + 16, h] for h in HALVES] for v in range(NVAR)]
            after_up = [[pltpu.roll(x, 7, 0) for x in pair] for pair in after]
        else:
            after, after_up = None, [[zero, zero]] * NVAR
        acc = [[src[u, s, rows, h] for h in HALVES] for u in range(NVAR)]
        for v in range(NVAR):
            x = here[v]
            down = [pltpu.roll(a, 1, 0) for a in x]
            right = [pltpu.roll(a, 1, 1) for a in x]
            left = [pltpu.roll(a, 127, 1) for a in x]
            nbs = (
                [p[v, s, rows, h] for h in HALVES],
                [p[v, s + 2, rows, h] for h in HALVES],
                [jnp.where(row == 0, a, b) for a, b in zip(below[v], down)],
                [jnp.where(row == 7, a, b) for a, b in zip(after_up[v], here_up[v])],
                [jnp.where(lane == 0, 0.0, right[0]), jnp.where(lane == 0, right[0], right[1])],
                [jnp.where(lane == 127, left[1], left[0]), jnp.where(lane == 127, 0.0, left[1])],
            )
            below[v] = down
            for d in range(6):
                for u in range(NVAR):
                    factor = coef[d * 25 + u * 5 + v]
                    for h in range(2):
                        acc[u][h] = acc[u][h] + factor * nbs[d][h]
        for u in range(NVAR):
            value = [invd[u, s, rows, HALVES[h]] * acc[u][h] for h in range(2)]
            for h in range(2):
                q[u, s + q_pad, rows, HALVES[h]] = value[h]
            if packed:
                both = place(lane, value[1], 127, face_lane(0, t, s), packed[u])
                packed[u] = place(lane, value[0], 0, face_lane(1, t, s), both)
        here, here_up = after, after_up
    return tuple(packed)


def kernel(coup, fmap, src_hbm, invd_hbm, wjac_hbm, weight_hbm, ids_hbm, out, sens, src, invd, wjac, weight, ids, coef,
           p0, p1, p2, fsend, fbuf0, fbuf1, fbuf2, wall, onehot, spread, acc, dense, pair, mine, landing,
           ld_sem, fs_sem, fr_sem, hs_sem, hr_sem, sw_sem, ds_sem, dr_sem):
    blk = lax.axis_index("blk")
    sub = lax.axis_index("sub")
    side, core = sub // 2, lax.rem(sub, 2)
    chip = blk * 2 + side
    lane1 = lax.broadcasted_iota(jnp.int32, (8, 128), 1)
    fields = (p0, p1, p2)
    fbufs = (fbuf0, fbuf1, fbuf2)

    def same_core(other):
        return (other // 2, lax.rem(other, 2) * 2 + core)

    loads = [
        pltpu.make_async_copy(a, b, ld_sem.at[i])
        for i, (a, b) in enumerate(((src_hbm, src), (invd_hbm, invd), (wjac_hbm, wjac), (weight_hbm, weight), (ids_hbm, ids)))
    ]
    for copy in loads:
        copy.start()

    barrier = pltpu.get_barrier_semaphore()

    def greet(d, c):
        pl.semaphore_signal(barrier, inc=1, device_id=same_core(lax.rem(chip + d, 64)), device_id_type=MESH)
        return c

    lax.fori_loop(1, 64, greet, 0)
    for step in (1, 3):
        pl.semaphore_signal(barrier, inc=1, device_id=(blk, lax.rem(sub + step, NSUB)), device_id_type=MESH)

    for d in range(6):
        for u in range(NVAR):
            for v in range(NVAR):
                coef[d * 25 + u * 5 + v] = jnp.full((8, 128), coup[0, d, u, v], jnp.float32)

    @pl.when(sub == 0)
    def _():
        for p in fields:
            p[:, 0] = jnp.zeros((NVAR, CK, CI), jnp.float32)

    @pl.when(sub == NSUB - 1)
    def _():
        for p in fields:
            p[:, CS + 1] = jnp.zeros((NVAR, CK, CI), jnp.float32)

    loads[0].wait()
    loads[1].wait()

    def first_row(s, packed):
        face, diag = list(packed[:NVAR]), list(packed[NVAR:])
        for v in range(NVAR):
            for t in range(KT):
                rows = slice(8 * t, 8 * t + 8)
                inv = invd[v, s, rows, :]
                value = inv * src[v, s, rows, :]
                p0[v, s + 1, rows, :] = value
                face[v] = place(lane1, value[:, 128:], 127, face_lane(0, t, s), face[v])
                face[v] = place(lane1, value[:, :128], 0, face_lane(1, t, s), face[v])
                diag[v] = place(lane1, inv[:, :128], 0, face_lane(0, t, s), diag[v])
                diag[v] = place(lane1, inv[:, 128:], 127, face_lane(1, t, s), diag[v])
        return tuple(face + diag)

    none = jnp.zeros((8, 128), jnp.float32)
    packed = lax.fori_loop(0, CS, first_row, (none,) * (2 * NVAR))
    face, diag = packed[:NVAR], packed[NVAR:]

    pl.semaphore_wait(barrier, 65)

    def up_copy(n):
        return pltpu.make_async_remote_copy(
            src_ref=fields[n].at[:, CS], dst_ref=fields[n].at[:, 0], send_sem=hs_sem.at[n, 0], recv_sem=hr_sem.at[n, 0],
            device_id=(blk, lax.rem(sub + 1, NSUB)), device_id_type=MESH)

    def down_copy(n):
        return pltpu.make_async_remote_copy(
            src_ref=fields[n].at[:, 1], dst_ref=fields[n].at[:, CS + 1], send_sem=hs_sem.at[n, 1], recv_sem=hr_sem.at[n, 1],
            device_id=(blk, lax.rem(sub + NSUB - 1, NSUB)), device_id_type=MESH)

    for n in range(SWEEPS):
        p = fields[n]
        fbuf = fbufs[n]
        last = n == SWEEPS - 1
        q, q_pad = (out, 0) if last else (fields[n + 1], 1)

        for v in range(NVAR):
            fsend[n, v] = face[v]
            fbuf[blk, v] = face[v]

        def send_face(d, c):
            target = lax.rem(blk + d, NBLK)
            pltpu.make_async_remote_copy(
                src_ref=fsend.at[n], dst_ref=fbuf.at[blk], send_sem=fs_sem.at[n], recv_sem=fr_sem.at[n],
                device_id=(target, sub), device_id_type=MESH).start()
            return c

        lax.fori_loop(1, NBLK, send_face, 0, unroll=31)

        if n > 0:
            def add_faces(s, c):
                for u in range(NVAR):
                    for t in range(KT):
                        rows = slice(8 * t, 8 * t + 8)
                        low = place(lane1, extra[u], face_lane(0, t, s), 0, 0.0)
                        high = place(lane1, extra[u], face_lane(1, t, s), 127, 0.0)
                        p[u, s + 1, rows, 0:128] = p[u, s + 1, rows, 0:128] + low
                        p[u, s + 1, rows, 128:256] = p[u, s + 1, rows, 128:256] + high
                return c

            lax.fori_loop(0, 2, lambda i, c: add_faces(i * (CS - 1), c), 0)
        pl.when(sub < NSUB - 1)(lambda: up_copy(n).start())
        pl.when(sub > 0)(lambda: down_copy(n).start())
        if n > 0:
            lax.fori_loop(1, CS - 1, add_faces, 0)

        faces0 = () if last else (none,) * NVAR
        step = lambda s, c: relax_row(s, p, q, q_pad, coef, src, invd, c)
        faces0 = lax.fori_loop(1, CS - 1, step, faces0)
        pl.when(sub > 0)(lambda: up_copy(n).wait_recv())
        pl.when(sub < NSUB - 1)(lambda: down_copy(n).wait_recv())
        faces0 = lax.fori_loop(0, 2, lambda i, c: step(i * (CS - 1), c), faces0)

        landed = fbuf.at[pl.ds(0, NBLK - 1)]
        pltpu.make_async_copy(landed, landed, fr_sem.at[n]).wait()
        low = fbuf[fmap[blk, 0]]
        high = fbuf[fmap[blk, 1]]
        from_low = lane1 < 64
        outer = [jnp.where(from_low, low[v], high[v]) for v in range(NVAR)]
        extra = []
        for u in range(NVAR):
            total = none
            for v in range(NVAR):
                total = total + jnp.where(from_low, coef[100 + u * 5 + v], coef[125 + u * 5 + v]) * outer[v]
            extra.append(diag[u] * total)
        if not last:
            face = [faces0[u] + pltpu.roll(extra[u], 64, 1) for u in range(NVAR)]

    def add_last(s, c):
        for u in range(NVAR):
            for t in range(KT):
                rows = slice(8 * t, 8 * t + 8)
                low = place(lane1, extra[u], face_lane(0, t, s), 0, 0.0)
                high = place(lane1, extra[u], face_lane(1, t, s), 127, 0.0)
                out[u, s, rows, 0:128] = out[u, s, rows, 0:128] + low
                out[u, s, rows, 128:256] = out[u, s, rows, 128:256] + high
        return c

    lax.fori_loop(0, CS, add_last, 0)
    for copy in loads[2:]:
        copy.wait()
    for c in range(3):
        total = jnp.zeros((CS, CI), jnp.float32)
        for v in range(NVAR):
            for k in range(2):
                total = total + wjac[c, v, k] * out[v, :, k, :]
        wall[c] = total

    acc[...] = jnp.zeros_like(acc)

    def slots(m, carry):
        point = ids[m]
        high = point >> 7
        holder = (high * 171) >> 9
        order = (holder & 1) * 64 + (holder >> 1)
        rank = jnp.where(point < 0, -1, (high - 3 * holder) * 128 + order)
        low = point & 127
        pieces = []
        for c in range(3):
            value = weight[m] * wall[c]
            top = value.astype(jnp.bfloat16).astype(jnp.float32)
            pieces.append(top)
            pieces.append(value - top)
        for s in range(CS):
            lanes = slice(s * CI, (s + 1) * CI)
            hit = lax.broadcasted_iota(jnp.int32, (384, CI), 0) == rank[s : s + 1, :]
            onehot[:, lanes] = jnp.where(hit, 1.0, 0.0).astype(jnp.bfloat16)
            match = lax.broadcasted_iota(jnp.int32, (128, CI), 0) == low[s : s + 1, :]
            for i in range(6):
                spread[i * 128 : (i + 1) * 128, lanes] = jnp.where(match, pieces[i][s : s + 1, :], 0.0).astype(jnp.bfloat16)
        acc[...] = acc[...] + lax.dot_general(
            onehot[...], spread[...], (((1,), (1,)), ((), ())), preferred_element_type=jnp.float32)
        return carry

    lax.fori_loop(0, 8, slots, 0)
    for j in range(3):
        for c in range(3):
            for g in range(16):
                rows = slice(j * 128 + g * 8, j * 128 + g * 8 + 8)
                total = acc[rows, c * 256 : c * 256 + 128] + acc[rows, c * 256 + 128 : c * 256 + 256]
                dense[pl.ds(g * 128 + c * 3 + j, 8, stride=16), :] = total

    swap = pltpu.make_async_remote_copy(
        src_ref=dense.at[pl.ds((1 - core) * 1024, 1024)], dst_ref=pair, send_sem=sw_sem.at[0], recv_sem=sw_sem.at[1],
        device_id=(blk, side * 2 + 1 - core), device_id_type=MESH)
    swap.start()
    swap.wait()

    def add(i, c):
        both = dense[pl.ds(core * 1024 + i * 16, 16), :] + pair[pl.ds(i * 16, 16), :]
        mine[i] = both[:9, :]
        return c

    lax.fori_loop(0, 64, add, 0, unroll=8)

    def send_points(d, c):
        other = lax.rem(chip + d, 64)
        pltpu.make_async_remote_copy(
            src_ref=mine.at[other], dst_ref=landing.at[d], send_sem=ds_sem, recv_sem=dr_sem,
            device_id=same_core(other), device_id_type=MESH).start()
        return c

    lax.fori_loop(1, 64, send_points, 0, unroll=9)
    landing[0] = mine[chip]
    landed = landing.at[pl.ds(1, 63)]
    pltpu.make_async_copy(landed, landed, dr_sem).wait()
    total = lax.fori_loop(0, 64, lambda i, t: t + landing[i], jnp.zeros((9, 128), jnp.float32), unroll=8)
    for c in range(3):
        for j in range(3):
            sens[c : c + 1, j * 128 : (j + 1) * 128] = total[c * 3 + j : c * 3 + j + 1, :]
    pltpu.make_async_copy(landed, landed, ds_sem).wait()

    for n in range(SWEEPS):
        pl.when(sub < NSUB - 1)(lambda n=n: up_copy(n).wait_send())
        pl.when(sub > 0)(lambda n=n: down_copy(n).wait_send())
        sent = fbufs[n].at[pl.ds(0, NBLK - 1)]
        pltpu.make_async_copy(sent, sent, fs_sem.at[n]).wait()


def body(source, inv_diag, coupling, face_map, wall_jac, ffd_weight, cp_ids):
    vmem = pl.BlockSpec(memory_space=pltpu.VMEM)
    smem = pl.BlockSpec(memory_space=pltpu.SMEM)
    hbm = pl.BlockSpec(memory_space=pl.ANY)
    f32, dma = jnp.float32, pltpu.SemaphoreType.DMA
    face_buffer = pltpu.VMEM((NBLK, NVAR, 8, 128), f32)
    field = pltpu.VMEM((NVAR, CS + 2, CK, CI), f32)
    return pl.pallas_call(
        kernel,
        out_shape=(jax.ShapeDtypeStruct((NVAR, CS, CK, CI), f32), jax.ShapeDtypeStruct((3, 384), f32)),
        in_specs=[smem, smem, hbm, hbm, hbm, hbm, hbm],
        out_specs=(vmem, vmem),
        scratch_shapes=[
            pltpu.VMEM((NVAR, CS, CK, CI), f32),
            pltpu.VMEM((NVAR, CS, CK, CI), f32),
            pltpu.VMEM((3, NVAR, 2, CS, CI), f32),
            pltpu.VMEM((8, CS, CI), f32),
            pltpu.VMEM((8, CS, CI), jnp.int32),
            pltpu.VMEM((150, 8, 128), f32),
            field,
            field,
            field,
            pltpu.VMEM((SWEEPS, NVAR, 8, 128), f32),
            face_buffer,
            face_buffer,
            face_buffer,
            pltpu.VMEM((3, CS, CI), f32),
            pltpu.VMEM((384, CS * CI), jnp.bfloat16),
            pltpu.VMEM((768, CS * CI), jnp.bfloat16),
            pltpu.VMEM((384, 768), f32),
            pltpu.VMEM((2048, 128), f32),
            pltpu.VMEM((1024, 128), f32),
            pltpu.VMEM((64, 9, 128), f32),
            pltpu.VMEM((64, 9, 128), f32),
            dma((5,)),
            dma((SWEEPS,)),
            dma((SWEEPS,)),
            dma((SWEEPS, 2)),
            dma((SWEEPS, 2)),
            dma((2,)),
            dma,
            dma,
        ],
        compiler_params=pltpu.CompilerParams(collective_id=0, has_side_effects=True, vmem_limit_bytes=56 << 20),
        name="adjoint",
    )(coupling, face_map, source, inv_diag, wall_jac, ffd_weight, cp_ids)


def solution(mesh):
    in_specs = (
        P(None, "sub", None, "blk"),
        P(None, "sub", None, "blk"),
        P("blk", None, None, None),
        P(),
        P(None, None, None, "sub", "blk"),
        P(None, "sub", "blk"),
        P(None, "sub", "blk"),
    )
    out_specs = (P(None, "sub", None, "blk"), P(None, ("blk", "sub")))
    return jax.shard_map(body, mesh=mesh, in_specs=in_specs, out_specs=out_specs, check_vma=False)
```

time: 128 us -> 84.1 us (0.66)
  Pallas kernels: 118 us -> 76.2 us
  local copies, waits for them, and re-layouts: 9.29 us -> 6.93 us
    pallas_call x3 -> x1, Pallas kernels: 118 us -> 76.2 us  [body(): pl.pallas_call(kernel, out_shape=(jax.ShapeDtypeStruct((NVAR, CS, CK, CI)...]
    unnamed x18 -> x6, local copies, waits for them, and re-layouts: 9.09 us -> 6.93 us
where the time goes in v2:
time: 84.1 us; the launch traced here: 83.8 us
  Pallas kernels  76.2 us (91%)
  local copies, waits for them, and re-layouts  6.93 us (8%)
    pallas_call x1, Pallas kernels, body(): pl.pallas_call(kernel, out_shape=(jax.ShapeDtypeStruct((NVAR, CS, CK, CI)...  76.2 us
    unnamed x6, local copies, waits for them, and re-layouts  6.93 us

profile of v2, /device:TPU:1, one launch (start us, length us, event | category | flops | bytes accessed | tf_op | source)
XLA Modules:
  0.0 83.8 jit_solution(10310274504326114060)
XLA Ops:
  0.6 1.4 %copy.10.fmap = s32[32,2]{1,0:T(8,128)} copy(s32[32,2]{0,1:T(2,128)} %param.10) | data formatting | bytes 512 | tf_op args[3]
  2.0 1.4 %copy.9.coup = f32[1,6,5,5]{3,2,1,0:T(8,128)} copy(f32[1,6,5,5]{1,0,3,2:T(1,128)} %param.9) | data formatting | bytes 1200 | tf_op args[2]
  3.4 76.2 %adjoint.1 = (f32[5,8,64,256]{3,2,1,0:T(8,128)}, f32[3,384]{1,0:T(4,128)}) custom-call(f32[1,6,5,5]{3,2,1,0:T(8,128)} %copy.9.coup, s32[32,2]{1,0:T(8,128)} %copy.10.fmap, f32[5,8,64,256]{3,2,1,0:T(8,128)} %src_hbm.1, f32[5,8,64,256]{3,2,1,0:T(8,128)} %invd_hbm.1, f32[3,5,2,8,256]{4,3,2,1,0:T(8,128)} %wjac_hbm.1, f32[8,8,256]{2,1,0:T(8,128)} %weight_hbm.1, ...), custom_call_target="tpu_custom_call" | custom-call | tf_op jit(solution)/shard_map/adjoint/pallas_call | solution.py:312
  79.7 0.0 copy-start
  79.7 3.5 %copy.13 = f32[5,8,64,256]{3,2,1,0:T(8,128)} copy(f32[5,8,64,256]{3,2,1,0:T(8,128)} %get-tuple-element.4) | data formatting | bytes 5242880
  83.2 0.0 copy-done
  83.2 0.6 copy.14
Async XLA Ops:
  79.7 3.6 %copy-start = (f32[3,384]{1,0:T(4,128)S(1)}, f32[3,384]{1,0:T(4,128)}, u32[]{:S(2)}) copy-start(f32[3,384]{1,0:T(4,128)} %get-tuple-element.5) | copy-start | bytes 13828

commit v3 on v2

--- a/solution.py
+++ b/solution.py
@@ -16,6 +16,7 @@
 NBLK = 32
 NSUB = 4
 KT = CK // 8
+SPAN_ROWS = ((0, 8), (8, CK - 8))
 HALVES = (slice(0, 128), slice(128, 256))
 
 
@@ -28,15 +29,19 @@
     return jnp.where(lane == target_lane, pltpu.roll(value, shift, 1), into)
 
 
-def relax_row(s, p, q, q_pad, coef, src, invd, packed):
+def relax_row(s, p, q, q_pad, coef, src, invd, packed, first=0, end=KT):
     row = lax.broadcasted_iota(jnp.int32, (8, 128), 0)
     lane = lax.broadcasted_iota(jnp.int32, (8, 128), 1)
     zero = jnp.zeros((8, 128), jnp.float32)
     packed = list(packed)
-    below = [[zero, zero] for _ in range(NVAR)]
-    here = [[p[v, s + 1, 0:8, h] for h in HALVES] for v in range(NVAR)]
+    if first:
+        edge = slice(8 * first - 8, 8 * first)
+        below = [[pltpu.roll(p[v, s + 1, edge, h], 1, 0) for h in HALVES] for v in range(NVAR)]
+    else:
+        below = [[zero, zero] for _ in range(NVAR)]
+    here = [[p[v, s + 1, 8 * first : 8 * first + 8, h] for h in HALVES] for v in range(NVAR)]
     here_up = [[pltpu.roll(x, 7, 0) for x in pair] for pair in here]
-    for t in range(KT):
+    for t in range(first, end):
         rows = slice(8 * t, 8 * t + 8)
         if t < KT - 1:
             after = [[p[v, s + 1, 8 * t + 8 : 8 * t + 16, h] for h in HALVES] for v in range(NVAR)]
@@ -108,7 +113,7 @@
     for d in range(6):
         for u in range(NVAR):
             for v in range(NVAR):
-                coef[d * 25 + u * 5 + v] = jnp.full((8, 128), coup[0, d, u, v], jnp.float32)
+                coef[d * 25 + u * 5 + v] = jnp.full((8, 128), coup[u, v, 0, d], jnp.float32)
 
     @pl.when(sub == 0)
     def _():
@@ -143,103 +148,130 @@
 
     pl.semaphore_wait(barrier, 65)
 
-    def up_copy(n):
+    def up_copy(n, i):
+        rows = pl.ds(*SPAN_ROWS[i])
         return pltpu.make_async_remote_copy(
-            src_ref=fields[n].at[:, CS], dst_ref=fields[n].at[:, 0], send_sem=hs_sem.at[n, 0], recv_sem=hr_sem.at[n, 0],
+            src_ref=fields[n].at[:, CS, rows], dst_ref=fields[n].at[:, 0, rows],
+            send_sem=hs_sem.at[n, 0, i], recv_sem=hr_sem.at[n, 0, i],
             device_id=(blk, lax.rem(sub + 1, NSUB)), device_id_type=MESH)
 
-    def down_copy(n):
+    def down_copy(n, i):
+        rows = pl.ds(*SPAN_ROWS[i])
         return pltpu.make_async_remote_copy(
-            src_ref=fields[n].at[:, 1], dst_ref=fields[n].at[:, CS + 1], send_sem=hs_sem.at[n, 1], recv_sem=hr_sem.at[n, 1],
+            src_ref=fields[n].at[:, 1, rows], dst_ref=fields[n].at[:, CS + 1, rows],
+            send_sem=hs_sem.at[n, 1, i], recv_sem=hr_sem.at[n, 1, i],
             device_id=(blk, lax.rem(sub + NSUB - 1, NSUB)), device_id_type=MESH)
 
-    for n in range(SWEEPS):
-        p = fields[n]
-        fbuf = fbufs[n]
-        last = n == SWEEPS - 1
-        q, q_pad = (out, 0) if last else (fields[n + 1], 1)
-
+    def start_spans(n):
+        for i in range(2):
+            pl.when(sub < NSUB - 1)(lambda: up_copy(n, i).start())
+            pl.when(sub > 0)(lambda: down_copy(n, i).start())
+
+    def spans_landed(n, i):
+        pl.when(sub > 0)(lambda: up_copy(n, i).wait_recv())
+        pl.when(sub < NSUB - 1)(lambda: down_copy(n, i).wait_recv())
+
+    def send_faces(n):
         for v in range(NVAR):
             fsend[n, v] = face[v]
-            fbuf[blk, v] = face[v]
+            fbufs[n][blk, v] = face[v]
 
         def send_face(d, c):
             target = lax.rem(blk + d, NBLK)
             pltpu.make_async_remote_copy(
-                src_ref=fsend.at[n], dst_ref=fbuf.at[blk], send_sem=fs_sem.at[n], recv_sem=fr_sem.at[n],
+                src_ref=fsend.at[n], dst_ref=fbufs[n].at[blk], send_sem=fs_sem.at[n], recv_sem=fr_sem.at[n],
                 device_id=(target, sub), device_id_type=MESH).start()
             return c
 
         lax.fori_loop(1, NBLK, send_face, 0, unroll=31)
 
-        if n > 0:
-            def add_faces(s, c):
-                for u in range(NVAR):
-                    for t in range(KT):
-                        rows = slice(8 * t, 8 * t + 8)
-                        low = place(lane1, extra[u], face_lane(0, t, s), 0, 0.0)
-                        high = place(lane1, extra[u], face_lane(1, t, s), 127, 0.0)
-                        p[u, s + 1, rows, 0:128] = p[u, s + 1, rows, 0:128] + low
-                        p[u, s + 1, rows, 128:256] = p[u, s + 1, rows, 128:256] + high
-                return c
-
-            lax.fori_loop(0, 2, lambda i, c: add_faces(i * (CS - 1), c), 0)
-        pl.when(sub < NSUB - 1)(lambda: up_copy(n).start())
-        pl.when(sub > 0)(lambda: down_copy(n).start())
-        if n > 0:
-            lax.fori_loop(1, CS - 1, add_faces, 0)
-
-        faces0 = () if last else (none,) * NVAR
-        step = lambda s, c: relax_row(s, p, q, q_pad, coef, src, invd, c)
-        faces0 = lax.fori_loop(1, CS - 1, step, faces0)
-        pl.when(sub > 0)(lambda: up_copy(n).wait_recv())
-        pl.when(sub < NSUB - 1)(lambda: down_copy(n).wait_recv())
-        faces0 = lax.fori_loop(0, 2, lambda i, c: step(i * (CS - 1), c), faces0)
-
+    def faces_landed(n):
+        fbuf = fbufs[n]
         landed = fbuf.at[pl.ds(0, NBLK - 1)]
         pltpu.make_async_copy(landed, landed, fr_sem.at[n]).wait()
-        low = fbuf[fmap[blk, 0]]
-        high = fbuf[fmap[blk, 1]]
+        low = fbuf[fmap[0, blk]]
+        high = fbuf[fmap[1, blk]]
         from_low = lane1 < 64
         outer = [jnp.where(from_low, low[v], high[v]) for v in range(NVAR)]
-        extra = []
+        terms = []
         for u in range(NVAR):
             total = none
             for v in range(NVAR):
                 total = total + jnp.where(from_low, coef[100 + u * 5 + v], coef[125 + u * 5 + v]) * outer[v]
-            extra.append(diag[u] * total)
-        if not last:
-            face = [faces0[u] + pltpu.roll(extra[u], 64, 1) for u in range(NVAR)]
-
-    def add_last(s, c):
+            terms.append(diag[u] * total)
+        return terms
+
+    def add_faces(p, pad, s, terms, tiles=(0, KT)):
         for u in range(NVAR):
-            for t in range(KT):
+            for t in range(*tiles):
                 rows = slice(8 * t, 8 * t + 8)
-                low = place(lane1, extra[u], face_lane(0, t, s), 0, 0.0)
-                high = place(lane1, extra[u], face_lane(1, t, s), 127, 0.0)
-                out[u, s, rows, 0:128] = out[u, s, rows, 0:128] + low
-                out[u, s, rows, 128:256] = out[u, s, rows, 128:256] + high
-        return c
-
-    lax.fori_loop(0, CS, add_last, 0)
+                low = place(lane1, terms[u], face_lane(0, t, s), 0, 0.0)
+                high = place(lane1, terms[u], face_lane(1, t, s), 127, 0.0)
+                p[u, s + pad, rows, 0:128] = p[u, s + pad, rows, 0:128] + low
+                p[u, s + pad, rows, 128:256] = p[u, s + pad, rows, 128:256] + high
+
+    def over(rows, step):
+        lo, hi = rows
+        lax.fori_loop(lo, hi, lambda s, c: (step(s), c)[1], 0)
+
+    def ends(step):
+        lax.fori_loop(0, 2, lambda i, c: (step(i * (CS - 1)), c)[1], 0)
+
+    for n in range(SWEEPS - 1):
+        p, q = fields[n], fields[n + 1]
+        send_faces(n)
+        if n > 0:
+            ends(lambda s: add_faces(p, 1, s, extra))
+        start_spans(n)
+        if n > 0:
+            over((1, CS - 1), lambda s: add_faces(p, 1, s, extra))
+        step = lambda s, c: relax_row(s, p, q, 1, coef, src, invd, c)
+        made = lax.fori_loop(1, CS - 1, step, (none,) * NVAR)
+        spans_landed(n, 0)
+        spans_landed(n, 1)
+        made = lax.fori_loop(0, 2, lambda i, c: step(i * (CS - 1), c), made)
+        extra = faces_landed(n)
+        face = [made[u] + pltpu.roll(extra[u], 64, 1) for u in range(NVAR)]
+
+    n = SWEEPS - 1
+    p = fields[n]
+    send_faces(n)
+    ends(lambda s: add_faces(p, 1, s, extra))
+    start_spans(n)
+    over((1, CS - 1), lambda s: add_faces(p, 1, s, extra))
+
+    def last_rows(s, first, end):
+        relax_row(s, p, out, 0, coef, src, invd, (), first, end)
+
+    over((1, CS - 1), lambda s: last_rows(s, 0, 1))
+    over((1, 3), lambda s: last_rows(s, 1, KT))
+    spans_landed(n, 0)
+    ends(lambda s: last_rows(s, 0, 1))
     for copy in loads[2:]:
         copy.wait()
-    for c in range(3):
+
+    def wall_of(c):
         total = jnp.zeros((CS, CI), jnp.float32)
         for v in range(NVAR):
             for k in range(2):
                 total = total + wjac[c, v, k] * out[v, :, k, :]
-        wall[c] = total
+        return total
+
+    column = lax.broadcasted_iota(jnp.int32, (CS, CI), 1)
+    inner = (column > 0) & (column < CI - 1)
+    for c in range(3):
+        wall[c] = jnp.where(inner, wall_of(c), 0.0)
 
     acc[...] = jnp.zeros_like(acc)
 
-    def slots(m, carry):
-        point = ids[m]
+    def row_and_lane(point):
         high = point >> 7
         holder = (high * 171) >> 9
         order = (holder & 1) * 64 + (holder >> 1)
-        rank = jnp.where(point < 0, -1, (high - 3 * holder) * 128 + order)
-        low = point & 127
+        return jnp.where(point < 0, -1, (high - 3 * holder) * 128 + order), point & 127
+
+    def slots(m, carry):
+        rank, low = row_and_lane(ids[m])
         pieces = []
         for c in range(3):
             value = weight[m] * wall[c]
@@ -258,6 +290,33 @@
         return carry
 
     lax.fori_loop(0, 8, slots, 0)
+
+    extra = faces_landed(n)
+    over((0, CS), lambda s: add_faces(out, 0, s, extra, (0, 1)))
+    walls = [wall_of(c) for c in range(3)]
+    marks = [jnp.full((8, 128), -1, jnp.int32), jnp.zeros((8, 128), jnp.int32)] + [none] * 3
+    for m in range(8):
+        rank, low = row_and_lane(ids[m])
+        for i, x in enumerate([rank, low] + [weight[m] * walls[c] for c in range(3)]):
+            marks[i] = place(lane1, x[:, :128], 0, 2 * m, marks[i])
+            marks[i] = place(lane1, x[:, 128:], 127, 2 * m + 1, marks[i])
+    line = lax.broadcasted_iota(jnp.int32, (1, 128), 1)
+    flat = []
+    for x in marks:
+        total = x[0:1, :]
+        for s in range(1, CS):
+            total = jnp.where((line >> 4) == s, pltpu.roll(x[s : s + 1, :], 16 * s, 1), total)
+        flat.append(total)
+    hit = lax.broadcasted_iota(jnp.int32, (384, 128), 0) == flat[0]
+    match = lax.broadcasted_iota(jnp.int32, (128, 128), 0) == flat[1]
+    edge_spread = []
+    for c in range(3):
+        top = flat[2 + c].astype(jnp.bfloat16).astype(jnp.float32)
+        for value in (top, flat[2 + c] - top):
+            edge_spread.append(jnp.where(match, value, 0.0).astype(jnp.bfloat16))
+    acc[...] = acc[...] + lax.dot_general(
+        jnp.where(hit, 1.0, 0.0).astype(jnp.bfloat16), jnp.concatenate(edge_spread, 0), (((1,), (1,)), ((), ())),
+        preferred_element_type=jnp.float32)
     for j in range(3):
         for c in range(3):
             for g in range(16):
@@ -287,6 +346,12 @@
 
     lax.fori_loop(1, 64, send_points, 0, unroll=9)
     landing[0] = mine[chip]
+
+    spans_landed(n, 1)
+    over((3, CS - 1), lambda s: last_rows(s, 1, KT))
+    ends(lambda s: last_rows(s, 1, KT))
+    over((0, CS), lambda s: add_faces(out, 0, s, extra, (1, KT)))
+
     landed = landing.at[pl.ds(1, 63)]
     pltpu.make_async_copy(landed, landed, dr_sem).wait()
     total = lax.fori_loop(0, 64, lambda i, t: t + landing[i], jnp.zeros((9, 128), jnp.float32), unroll=8)
@@ -296,8 +361,9 @@
     pltpu.make_async_copy(landed, landed, ds_sem).wait()
 
     for n in range(SWEEPS):
-        pl.when(sub < NSUB - 1)(lambda n=n: up_copy(n).wait_send())
-        pl.when(sub > 0)(lambda n=n: down_copy(n).wait_send())
+        for i in range(2):
+            pl.when(sub < NSUB - 1)(lambda: up_copy(n, i).wait_send())
+            pl.when(sub > 0)(lambda: down_copy(n, i).wait_send())
         sent = fbufs[n].at[pl.ds(0, NBLK - 1)]
         pltpu.make_async_copy(sent, sent, fs_sem.at[n]).wait()
 
@@ -305,7 +371,7 @@
 def body(source, inv_diag, coupling, face_map, wall_jac, ffd_weight, cp_ids):
     vmem = pl.BlockSpec(memory_space=pltpu.VMEM)
     smem = pl.BlockSpec(memory_space=pltpu.SMEM)
-    hbm = pl.BlockSpec(memory_space=pl.ANY)
+    hbm = pl.BlockSpec(memory_space=pltpu.HBM)
     f32, dma = jnp.float32, pltpu.SemaphoreType.DMA
     face_buffer = pltpu.VMEM((NBLK, NVAR, 8, 128), f32)
     field = pltpu.VMEM((NVAR, CS + 2, CK, CI), f32)
@@ -339,15 +405,15 @@
             dma((5,)),
             dma((SWEEPS,)),
             dma((SWEEPS,)),
-            dma((SWEEPS, 2)),
-            dma((SWEEPS, 2)),
+            dma((SWEEPS, 2, 2)),
+            dma((SWEEPS, 2, 2)),
             dma((2,)),
             dma,
             dma,
         ],
-        compiler_params=pltpu.CompilerParams(collective_id=0, has_side_effects=True, vmem_limit_bytes=56 << 20),
+        compiler_params=pltpu.CompilerParams(collective_id=0, has_side_effects=True, vmem_limit_bytes=40 << 20),
         name="adjoint",
-    )(coupling, face_map, source, inv_diag, wall_jac, ffd_weight, cp_ids)
+    )(jnp.transpose(coupling, (2, 3, 0, 1)), face_map.T, source, inv_diag, wall_jac, ffd_weight, cp_ids)
 
 
 def solution(mesh):

time: 84.1 us -> 82.9 us (0.986)
  Pallas kernels: 76.2 us -> 72.3 us
  local copies, waits for them, and re-layouts: 6.93 us -> 9.57 us
    pallas_call x1, Pallas kernels: 76.2 us -> 72.3 us  [body(): pl.pallas_call(kernel, out_shape=(jax.ShapeDtypeStruct((NVAR, CS, CK, CI)...]
    unnamed x6 -> x16, local copies, waits for them, and re-layouts: 6.93 us -> 9.57 us
where the time goes in v3:
time: 82.9 us; the launch traced here: 82.5 us
  Pallas kernels  72.3 us (87%)
  local copies, waits for them, and re-layouts  9.57 us (12%)
    pallas_call x1, Pallas kernels, body(): pl.pallas_call(kernel, out_shape=(jax.ShapeDtypeStruct((NVAR, CS, CK, CI)...  72.3 us
    unnamed x16, local copies, waits for them, and re-layouts  9.57 us

profile of v3, /device:TPU:1, one launch (start us, length us, event | category | flops | bytes accessed | tf_op | source)
XLA Modules:
  0.0 82.5 jit_solution(9514420763848694347)
XLA Ops:
  0.6 0.0 copy-start
  0.6 1.7 %copy-done = f32[5,8,64,256]{3,2,1,0:T(8,128)S(1)} copy-done((f32[5,8,64,256]{3,2,1,0:T(8,128)S(1)}, f32[5,8,64,256]{3,2,1,0:T(8,128)}, u32[]{:S(2)}) %copy-start) | copy-done | bytes 2621464
  2.4 0.0 copy-start.1
  2.4 1.7 %copy-done.1 = f32[5,8,64,256]{3,2,1,0:T(8,128)S(1)} copy-done((f32[5,8,64,256]{3,2,1,0:T(8,128)S(1)}, f32[5,8,64,256]{3,2,1,0:T(8,128)}, u32[]{:S(2)}) %copy-start.1) | copy-done | bytes 2621464
  4.1 0.0 copy-start.2
  4.1 0.9 %copy-done.2 = f32[3,5,2,8,256]{4,3,2,1,0:T(8,128)S(1)} copy-done((f32[3,5,2,8,256]{4,3,2,1,0:T(8,128)S(1)}, f32[3,5,2,8,256]{4,3,2,1,0:T(8,128)}, u32[]{:S(2)}) %copy-start.2) | copy-done | bytes 245784
  5.1 0.0 copy-start.3
  5.1 0.8 %copy-done.3 = f32[8,8,256]{2,1,0:T(8,128)S(1)} copy-done((f32[8,8,256]{2,1,0:T(8,128)S(1)}, f32[8,8,256]{2,1,0:T(8,128)}, u32[]{:S(2)}) %copy-start.3) | copy-done | bytes 65560
  5.9 0.0 copy-start.4
  5.9 0.8 %copy-done.4 = s32[8,8,256]{2,1,0:T(8,128)S(1)} copy-done((s32[8,8,256]{2,1,0:T(8,128)S(1)}, s32[8,8,256]{2,1,0:T(8,128)}, u32[]{:S(2)}) %copy-start.4) | copy-done | bytes 65560
  6.7 0.0 copy-start.5
  6.7 0.7 copy-done.5
  7.4 0.0 copy-start.6
  7.4 0.7 copy-done.6
  8.1 72.3 %adjoint.1 = (f32[5,8,64,256]{3,2,1,0:T(8,128)S(1)}, f32[3,384]{1,0:T(4,128)S(1)}) custom-call(f32[5,5,1,6]{3,2,1,0:T(1,128)S(1)} %bitcast.2, s32[2,32]{1,0:T(2,128)S(1)} %bitcast.3, f32[5,8,64,256]{3,2,1,0:T(8,128)S(1)} %copy-done, f32[5,8,64,256]{3,2,1,0:T(8,128)S(1)} %copy-done.1, f32[3,5,2,8,256]{4,3,2,1,0:T(8,128)S(1)} %copy-done.2, ...), custom_call_target="tpu_custom_call" | custom-call | tf_op jit(solution)/shard_map/adjoint/pallas_call | solution.py:378
  80.4 1.5 %copy.11 = f32[5,8,64,256]{3,2,1,0:T(8,128)} copy(f32[5,8,64,256]{3,2,1,0:T(8,128)S(1)} %get-tuple-element.4) | data formatting | bytes 5242880
  81.9 0.6 copy.12
Async XLA Ops:
  0.6 1.7 %copy-start = (f32[5,8,64,256]{3,2,1,0:T(8,128)S(1)}, f32[5,8,64,256]{3,2,1,0:T(8,128)}, u32[]{:S(2)}) copy-start(f32[5,8,64,256]{3,2,1,0:T(8,128)} %src_hbm.1) | copy-start | bytes 7864324
  2.4 1.7 %copy-start.1 = (f32[5,8,64,256]{3,2,1,0:T(8,128)S(1)}, f32[5,8,64,256]{3,2,1,0:T(8,128)}, u32[]{:S(2)}) copy-start(f32[5,8,64,256]{3,2,1,0:T(8,128)} %invd_hbm.1) | copy-start | bytes 7864324
  4.1 0.9 %copy-start.2 = (f32[3,5,2,8,256]{4,3,2,1,0:T(8,128)S(1)}, f32[3,5,2,8,256]{4,3,2,1,0:T(8,128)}, u32[]{:S(2)}) copy-start(f32[3,5,2,8,256]{4,3,2,1,0:T(8,128)} %wjac_hbm.1) | copy-start | bytes 737284
  5.1 0.8 %copy-start.3 = (f32[8,8,256]{2,1,0:T(8,128)S(1)}, f32[8,8,256]{2,1,0:T(8,128)}, u32[]{:S(2)}) copy-start(f32[8,8,256]{2,1,0:T(8,128)} %weight_hbm.1) | copy-start | bytes 196612
  5.9 0.8 %copy-start.4 = (s32[8,8,256]{2,1,0:T(8,128)S(1)}, s32[8,8,256]{2,1,0:T(8,128)}, u32[]{:S(2)}) copy-start(s32[8,8,256]{2,1,0:T(8,128)} %ids_hbm.1) | copy-start | bytes 196612
  6.7 0.7 copy-start.5
  7.4 0.7 copy-start.6

commit v4 on v3

--- a/solution.py
+++ b/solution.py
@@ -79,7 +79,7 @@
     return tuple(packed)
 
 
-def kernel(coup, fmap, src_hbm, invd_hbm, wjac_hbm, weight_hbm, ids_hbm, out, sens, src, invd, wjac, weight, ids, coef,
+def kernel(coup_hbm, fmap_hbm, src_hbm, invd_hbm, wjac_hbm, weight_hbm, ids_hbm, out, sens, coup, fmap, src, invd, wjac, weight, ids, coef,
            p0, p1, p2, fsend, fbuf0, fbuf1, fbuf2, wall, onehot, spread, acc, dense, pair, mine, landing,
            ld_sem, fs_sem, fr_sem, hs_sem, hr_sem, sw_sem, ds_sem, dr_sem):
     blk = lax.axis_index("blk")
@@ -95,7 +95,8 @@
 
     loads = [
         pltpu.make_async_copy(a, b, ld_sem.at[i])
-        for i, (a, b) in enumerate(((src_hbm, src), (invd_hbm, invd), (wjac_hbm, wjac), (weight_hbm, weight), (ids_hbm, ids)))
+        for i, (a, b) in enumerate((
+            (coup_hbm, coup), (fmap_hbm, fmap), (src_hbm, src), (invd_hbm, invd), (wjac_hbm, wjac), (weight_hbm, weight), (ids_hbm, ids)))
     ]
     for copy in loads:
         copy.start()
@@ -110,6 +111,8 @@
     for step in (1, 3):
         pl.semaphore_signal(barrier, inc=1, device_id=(blk, lax.rem(sub + step, NSUB)), device_id_type=MESH)
 
+    loads[0].wait()
+    loads[1].wait()
     for d in range(6):
         for u in range(NVAR):
             for v in range(NVAR):
@@ -125,8 +128,8 @@
         for p in fields:
             p[:, CS + 1] = jnp.zeros((NVAR, CK, CI), jnp.float32)
 
-    loads[0].wait()
-    loads[1].wait()
+    loads[2].wait()
+    loads[3].wait()
 
     def first_row(s, packed):
         face, diag = list(packed[:NVAR]), list(packed[NVAR:])
@@ -247,7 +250,7 @@
     over((1, 3), lambda s: last_rows(s, 1, KT))
     spans_landed(n, 0)
     ends(lambda s: last_rows(s, 0, 1))
-    for copy in loads[2:]:
+    for copy in loads[4:]:
         copy.wait()
 
     def wall_of(c):
@@ -370,17 +373,19 @@
 
 def body(source, inv_diag, coupling, face_map, wall_jac, ffd_weight, cp_ids):
     vmem = pl.BlockSpec(memory_space=pltpu.VMEM)
-    smem = pl.BlockSpec(memory_space=pltpu.SMEM)
     hbm = pl.BlockSpec(memory_space=pltpu.HBM)
     f32, dma = jnp.float32, pltpu.SemaphoreType.DMA
+    args = (jnp.transpose(coupling, (2, 3, 0, 1)), face_map.T, source, inv_diag, wall_jac, ffd_weight, cp_ids)
     face_buffer = pltpu.VMEM((NBLK, NVAR, 8, 128), f32)
     field = pltpu.VMEM((NVAR, CS + 2, CK, CI), f32)
     return pl.pallas_call(
         kernel,
         out_shape=(jax.ShapeDtypeStruct((NVAR, CS, CK, CI), f32), jax.ShapeDtypeStruct((3, 384), f32)),
-        in_specs=[smem, smem, hbm, hbm, hbm, hbm, hbm],
+        in_specs=[hbm] * 7,
         out_specs=(vmem, vmem),
         scratch_shapes=[
+            pltpu.SMEM((NVAR, NVAR, 1, 6), f32),
+            pltpu.SMEM((2, NBLK), jnp.int32),
             pltpu.VMEM((NVAR, CS, CK, CI), f32),
             pltpu.VMEM((NVAR, CS, CK, CI), f32),
             pltpu.VMEM((3, NVAR, 2, CS, CI), f32),
@@ -402,7 +407,7 @@
             pltpu.VMEM((1024, 128), f32),
             pltpu.VMEM((64, 9, 128), f32),
             pltpu.VMEM((64, 9, 128), f32),
-            dma((5,)),
+            dma((7,)),
             dma((SWEEPS,)),
             dma((SWEEPS,)),
             dma((SWEEPS, 2, 2)),
@@ -413,7 +418,7 @@
         ],
         compiler_params=pltpu.CompilerParams(collective_id=0, has_side_effects=True, vmem_limit_bytes=40 << 20),
         name="adjoint",
-    )(jnp.transpose(coupling, (2, 3, 0, 1)), face_map.T, source, inv_diag, wall_jac, ffd_weight, cp_ids)
+    )(*[pltpu.with_memory_space_constraint(x, pltpu.HBM) for x in args])
 
 
 def solution(mesh):

time: 82.9 us -> 73.5 us (0.89)
  local copies, waits for them, and re-layouts: 9.57 us -> 2.09 us
  Pallas kernels: 72.3 us -> 70.7 us
    unnamed x16 -> x2, local copies, waits for them, and re-layouts: 9.57 us -> 2.09 us
    pallas_call x1, Pallas kernels: 72.3 us -> 70.7 us  [body(): pl.pallas_call(kernel, out_shape=(jax.ShapeDtypeStruct((NVAR, CS, CK, CI)...]
where the time goes in v4:
time: 73.5 us; the launch traced here: 73.4 us
  Pallas kernels  70.7 us (96%)
  local copies, waits for them, and re-layouts  2.09 us (3%)
    pallas_call x1, Pallas kernels, body(): pl.pallas_call(kernel, out_shape=(jax.ShapeDtypeStruct((NVAR, CS, CK, CI)...  70.7 us
    unnamed x2, local copies, waits for them, and re-layouts  2.09 us

profile of v4, /device:TPU:1, one launch (start us, length us, event | category | flops | bytes accessed | tf_op | source)
XLA Modules:
  0.0 73.4 jit_solution(17570358472472472832)
XLA Ops:
  0.6 70.7 %adjoint.1 = (f32[5,8,64,256]{3,2,1,0:T(8,128)S(1)}, f32[3,384]{1,0:T(4,128)S(1)}) custom-call(f32[5,5,1,6]{3,2,1,0:T(1,128)} %bitcast.2, s32[2,32]{1,0:T(2,128)} %bitcast.3, f32[5,8,64,256]{3,2,1,0:T(8,128)} %src_hbm.1, f32[5,8,64,256]{3,2,1,0:T(8,128)} %invd_hbm.1, f32[3,5,2,8,256]{4,3,2,1,0:T(8,128)} %wjac_hbm.1, f32[8,8,256]{2,1,0:T(8,128)} %weight_hbm.1, ...), custom_call_target="tpu_custom_call" | custom-call | tf_op jit(solution)/shard_map/adjoint/pallas_call | solution.py:381
  71.3 1.5 %copy.11 = f32[5,8,64,256]{3,2,1,0:T(8,128)} copy(f32[5,8,64,256]{3,2,1,0:T(8,128)S(1)} %get-tuple-element.4) | data formatting | bytes 5242880
  72.8 0.6 copy.12

commit v5 on v4

--- a/solution.py
+++ b/solution.py
@@ -18,6 +18,16 @@
 KT = CK // 8
 SPAN_ROWS = ((0, 8), (8, CK - 8))
 HALVES = (slice(0, 128), slice(128, 256))
+
+
+def hops(offset):
+    dh, dx, dz, dl = offset
+    return (0, 1, 2, 1)[dx] + (0, 1, 2, 1)[dz] + (2 * (1 - dl) if dh else dl) + (dh * dl)
+
+
+CHIPS = [(dh, dx, dz, dl) for dh in range(2) for dx in range(4) for dz in range(4) for dl in range(2)]
+FAR_CHIPS = sorted(CHIPS[1:], key=lambda offset: -hops(offset))
+FAR_BLOCKS = [offset for offset in FAR_CHIPS if not offset[3]]
 
 
 def face_lane(half, tile, row):
@@ -90,8 +100,16 @@
     fields = (p0, p1, p2)
     fbufs = (fbuf0, fbuf1, fbuf2)
 
-    def same_core(other):
-        return (other // 2, lax.rem(other, 2) * 2 + core)
+    high_y, at_x, at_z = lax.div(blk, 16), lax.rem(lax.div(blk, 4), 4), lax.rem(blk, 4)
+
+    def moved(offset):
+        dh, dx, dz, dl = offset
+        other = lax.rem(high_y + dh, 2) * 16 + lax.rem(at_x + dx, 4) * 4 + lax.rem(at_z + dz, 4)
+        return other, lax.rem(side + dl, 2)
+
+    def same_core(offset):
+        other, other_side = moved(offset)
+        return (other, other_side * 2 + core)
 
     loads = [
         pltpu.make_async_copy(a, b, ld_sem.at[i])
@@ -103,11 +121,8 @@
 
     barrier = pltpu.get_barrier_semaphore()
 
-    def greet(d, c):
-        pl.semaphore_signal(barrier, inc=1, device_id=same_core(lax.rem(chip + d, 64)), device_id_type=MESH)
-        return c
-
-    lax.fori_loop(1, 64, greet, 0)
+    for offset in FAR_CHIPS:
+        pl.semaphore_signal(barrier, inc=1, device_id=same_core(offset), device_id_type=MESH)
     for step in (1, 3):
         pl.semaphore_signal(barrier, inc=1, device_id=(blk, lax.rem(sub + step, NSUB)), device_id_type=MESH)
 
@@ -179,14 +194,10 @@
             fsend[n, v] = face[v]
             fbufs[n][blk, v] = face[v]
 
-        def send_face(d, c):
-            target = lax.rem(blk + d, NBLK)
+        for offset in FAR_BLOCKS:
             pltpu.make_async_remote_copy(
                 src_ref=fsend.at[n], dst_ref=fbufs[n].at[blk], send_sem=fs_sem.at[n], recv_sem=fr_sem.at[n],
-                device_id=(target, sub), device_id_type=MESH).start()
-            return c
-
-        lax.fori_loop(1, NBLK, send_face, 0, unroll=31)
+                device_id=same_core(offset), device_id_type=MESH).start()
 
     def faces_landed(n):
         fbuf = fbufs[n]
@@ -273,26 +284,28 @@
         order = (holder & 1) * 64 + (holder >> 1)
         return jnp.where(point < 0, -1, (high - 3 * holder) * 128 + order), point & 127
 
-    def slots(m, carry):
-        rank, low = row_and_lane(ids[m])
-        pieces = []
-        for c in range(3):
-            value = weight[m] * wall[c]
-            top = value.astype(jnp.bfloat16).astype(jnp.float32)
-            pieces.append(top)
-            pieces.append(value - top)
-        for s in range(CS):
-            lanes = slice(s * CI, (s + 1) * CI)
-            hit = lax.broadcasted_iota(jnp.int32, (384, CI), 0) == rank[s : s + 1, :]
-            onehot[:, lanes] = jnp.where(hit, 1.0, 0.0).astype(jnp.bfloat16)
-            match = lax.broadcasted_iota(jnp.int32, (128, CI), 0) == low[s : s + 1, :]
-            for i in range(6):
-                spread[i * 128 : (i + 1) * 128, lanes] = jnp.where(match, pieces[i][s : s + 1, :], 0.0).astype(jnp.bfloat16)
+    def slots(step, carry):
+        for i in range(2):
+            m = 2 * step + i
+            rank, low = row_and_lane(ids[m])
+            pieces = []
+            for c in range(3):
+                value = weight[m] * wall[c]
+                top = value.astype(jnp.bfloat16).astype(jnp.float32)
+                pieces.append(top)
+                pieces.append(value - top)
+            for s in range(CS):
+                lanes = slice((i * CS + s) * CI, (i * CS + s + 1) * CI)
+                hit = lax.broadcasted_iota(jnp.int32, (384, CI), 0) == rank[s : s + 1, :]
+                onehot[:, lanes] = jnp.where(hit, 1.0, 0.0).astype(jnp.bfloat16)
+                match = lax.broadcasted_iota(jnp.int32, (128, CI), 0) == low[s : s + 1, :]
+                for k in range(6):
+                    spread[k * 128 : (k + 1) * 128, lanes] = jnp.where(match, pieces[k][s : s + 1, :], 0.0).astype(jnp.bfloat16)
         acc[...] = acc[...] + lax.dot_general(
             onehot[...], spread[...], (((1,), (1,)), ((), ())), preferred_element_type=jnp.float32)
         return carry
 
-    lax.fori_loop(0, 8, slots, 0)
+    lax.fori_loop(0, 4, slots, 0)
 
     extra = faces_landed(n)
     over((0, CS), lambda s: add_faces(out, 0, s, extra, (0, 1)))
@@ -340,14 +353,11 @@
 
     lax.fori_loop(0, 64, add, 0, unroll=8)
 
-    def send_points(d, c):
-        other = lax.rem(chip + d, 64)
+    for d, offset in enumerate(FAR_CHIPS):
+        other, other_side = moved(offset)
         pltpu.make_async_remote_copy(
-            src_ref=mine.at[other], dst_ref=landing.at[d], send_sem=ds_sem, recv_sem=dr_sem,
-            device_id=same_core(other), device_id_type=MESH).start()
-        return c
-
-    lax.fori_loop(1, 64, send_points, 0, unroll=9)
+            src_ref=mine.at[other * 2 + other_side], dst_ref=landing.at[d + 1], send_sem=ds_sem, recv_sem=dr_sem,
+            device_id=same_core(offset), device_id_type=MESH).start()
     landing[0] = mine[chip]
 
     spans_landed(n, 1)
@@ -400,8 +410,8 @@
             face_buffer,
             face_buffer,
             pltpu.VMEM((3, CS, CI), f32),
-            pltpu.VMEM((384, CS * CI), jnp.bfloat16),
-            pltpu.VMEM((768, CS * CI), jnp.bfloat16),
+            pltpu.VMEM((384, 2 * CS * CI), jnp.bfloat16),
+            pltpu.VMEM((768, 2 * CS * CI), jnp.bfloat16),
             pltpu.VMEM((384, 768), f32),
             pltpu.VMEM((2048, 128), f32),
             pltpu.VMEM((1024, 128), f32),
@@ -416,7 +426,7 @@
             dma,
             dma,
         ],
-        compiler_params=pltpu.CompilerParams(collective_id=0, has_side_effects=True, vmem_limit_bytes=40 << 20),
+        compiler_params=pltpu.CompilerParams(collective_id=0, has_side_effects=True, vmem_limit_bytes=44 << 20),
         name="adjoint",
     )(*[pltpu.with_memory_space_constraint(x, pltpu.HBM) for x in args])
 

time: 73.5 us -> 71.6 us (0.974)
  Pallas kernels: 70.7 us -> 68.7 us
    pallas_call x1, Pallas kernels: 70.7 us -> 68.7 us  [body(): pl.pallas_call(kernel, out_shape=(jax.ShapeDtypeStruct((NVAR, CS, CK, CI)...]
where the time goes in v5:
time: 71.6 us; the launch traced here: 71.4 us
  Pallas kernels  68.7 us (96%)
  local copies, waits for them, and re-layouts  2.09 us (3%)
    pallas_call x1, Pallas kernels, body(): pl.pallas_call(kernel, out_shape=(jax.ShapeDtypeStruct((NVAR, CS, CK, CI)...  68.7 us
    unnamed x2, local copies, waits for them, and re-layouts  2.09 us

profile of v5, /device:TPU:1, one launch (start us, length us, event | category | flops | bytes accessed | tf_op | source)
XLA Modules:
  0.0 71.4 jit_solution(4025051590277184794)
XLA Ops:
  0.6 68.7 %adjoint.1 = (f32[5,8,64,256]{3,2,1,0:T(8,128)S(1)}, f32[3,384]{1,0:T(4,128)S(1)}) custom-call(f32[5,5,1,6]{3,2,1,0:T(1,128)} %bitcast.2, s32[2,32]{1,0:T(2,128)} %bitcast.3, f32[5,8,64,256]{3,2,1,0:T(8,128)} %src_hbm.1, f32[5,8,64,256]{3,2,1,0:T(8,128)} %invd_hbm.1, f32[3,5,2,8,256]{4,3,2,1,0:T(8,128)} %wjac_hbm.1, f32[8,8,256]{2,1,0:T(8,128)} %weight_hbm.1, ...), custom_call_target="tpu_custom_call" | custom-call | tf_op jit(solution)/shard_map/adjoint/pallas_call | solution.py:391
  69.4 1.5 %copy.11 = f32[5,8,64,256]{3,2,1,0:T(8,128)} copy(f32[5,8,64,256]{3,2,1,0:T(8,128)S(1)} %get-tuple-element.4) | data formatting | bytes 5242880
  70.9 0.6 copy.12

commit v6 on v5

--- a/solution.py
+++ b/solution.py
@@ -344,6 +344,7 @@
         src_ref=dense.at[pl.ds((1 - core) * 1024, 1024)], dst_ref=pair, send_sem=sw_sem.at[0], recv_sem=sw_sem.at[1],
         device_id=(blk, side * 2 + 1 - core), device_id_type=MESH)
     swap.start()
+    over((3, 5), lambda s: last_rows(s, 1, KT))
     swap.wait()
 
     def add(i, c):
@@ -361,7 +362,7 @@
     landing[0] = mine[chip]
 
     spans_landed(n, 1)
-    over((3, CS - 1), lambda s: last_rows(s, 1, KT))
+    over((5, CS - 1), lambda s: last_rows(s, 1, KT))
     ends(lambda s: last_rows(s, 1, KT))
     over((0, CS), lambda s: add_faces(out, 0, s, extra, (1, KT)))
 

time: 71.6 us -> 70.9 us (level)
  no operation moved by 1% of the time
where the time goes in v6:
time: 70.9 us; the launch traced here: 70.8 us
  Pallas kernels  68.1 us (96%)
  local copies, waits for them, and re-layouts  2.09 us (3%)
    pallas_call x1, Pallas kernels, body(): pl.pallas_call(kernel, out_shape=(jax.ShapeDtypeStruct((NVAR, CS, CK, CI)...  68.1 us
    unnamed x2, local copies, waits for them, and re-layouts  2.09 us

profile of v6, /device:TPU:1, one launch (start us, length us, event | category | flops | bytes accessed | tf_op | source)
XLA Modules:
  0.0 70.8 jit_solution(4051860885442489388)
XLA Ops:
  0.6 68.1 %adjoint.1 = (f32[5,8,64,256]{3,2,1,0:T(8,128)S(1)}, f32[3,384]{1,0:T(4,128)S(1)}) custom-call(f32[5,5,1,6]{3,2,1,0:T(1,128)} %bitcast.2, s32[2,32]{1,0:T(2,128)} %bitcast.3, f32[5,8,64,256]{3,2,1,0:T(8,128)} %src_hbm.1, f32[5,8,64,256]{3,2,1,0:T(8,128)} %invd_hbm.1, f32[3,5,2,8,256]{4,3,2,1,0:T(8,128)} %wjac_hbm.1, f32[8,8,256]{2,1,0:T(8,128)} %weight_hbm.1, ...), custom_call_target="tpu_custom_call" | custom-call | tf_op jit(solution)/shard_map/adjoint/pallas_call | solution.py:392
  68.7 1.5 %copy.11 = f32[5,8,64,256]{3,2,1,0:T(8,128)} copy(f32[5,8,64,256]{3,2,1,0:T(8,128)S(1)} %get-tuple-element.4) | data formatting | bytes 5242880
  70.2 0.6 copy.12
